TPU v7x, 32 devices: a whole 2x2x4 slice. The times are simulated.
32 devices in a mesh: dp: 4 (over y, core), ctx: 4 (over z), tensor: 2 (over x).
Axes of the slice: x: 2, y: 2, z: 4, core: 2. Of those that a mesh axis runs over, the one named last changes fastest.
Arguments:
- block_input: float32 [1536, 12, 768], P(('ctx', 'tensor'), 'dp'), may hold values from -6 to 6
- out_cotangent: float32 [1536, 12, 768], P(('ctx', 'tensor'), 'dp'), may hold values from -6 to 6
- qkv_weight: float32 [768, 3, 768], P(('dp', 'ctx'), None, 'tensor'), may hold values from -0.21875 to 0.21875
- proj_weight: float32 [768, 768], P(('dp', 'ctx'), 'tensor'), may hold values from -4 to 4
- up_weight: float32 [768, 3072], P(('dp', 'ctx'), 'tensor'), may hold values from -0.21875 to 0.21875
- down_weight: float32 [768, 3072], P(('dp', 'ctx'), 'tensor'), may hold values from -0.109375 to 0.109375
- norm_gains: float32 [2, 768], P(None, ('dp', 'ctx')), may hold values from 0.1 to 1.9
- shift_terms: float32 [4, 768], P(None, ('dp', 'ctx')), may hold values from -1.5 to 1.5
- qv_bias: float32 [2, 12, 64], P(None, 'tensor', ('dp', 'ctx')), may hold values from -1.5 to 1.5
- up_bias: float32 [24, 128], P('tensor', ('dp', 'ctx')), may hold values from -1.5 to 1.5
- qkv_first: float32 [768, 3, 768], P(('dp', 'ctx'), None, 'tensor'), may hold values from -64 to 64
- qkv_second: float32 [768, 3, 768], P(('dp', 'ctx'), None, 'tensor'), may hold values from 13824 to 55296
- proj_first: float32 [768, 768], P(('dp', 'ctx'), 'tensor'), may hold values from -20 to 20
- proj_second: float32 [768, 768], P(('dp', 'ctx'), 'tensor'), may hold values from 44.2368 to 176.9472
- up_first: float32 [768, 3072], P(('dp', 'ctx'), 'tensor'), may hold values from -40 to 40
- up_second: float32 [768, 3072], P(('dp', 'ctx'), 'tensor'), may hold values from 129.024 to 516.096
- down_first: float32 [768, 3072], P(('dp', 'ctx'), 'tensor'), may hold values from -40 to 40
- down_second: float32 [768, 3072], P(('dp', 'ctx'), 'tensor'), may hold values from 221.184 to 884.736
- gains_first: float32 [2, 768], P(None, ('dp', 'ctx'))
- gains_second: float32 [2, 768], P(None, ('dp', 'ctx'))
- shifts_first: float32 [4, 768], P(None, ('dp', 'ctx'))
- shifts_second: float32 [4, 768], P(None, ('dp', 'ctx'))
- qv_bias_first: float32 [2, 12, 64], P(None, 'tensor', ('dp', 'ctx')), may hold values from -64 to 64
- qv_bias_second: float32 [2, 12, 64], P(None, 'tensor', ('dp', 'ctx')), may hold values from 1382400 to 5529600
- up_bias_first: float32 [24, 128], P('tensor', ('dp', 'ctx')), may hold values from -40 to 40
- up_bias_second: float32 [24, 128], P('tensor', ('dp', 'ctx')), may hold values from 23.04 to 92.16
Outputs:
- block_output: float32 [1536, 12, 768], P(('ctx', 'tensor'), 'dp')
- input_grad: float32 [1536, 12, 768], P(('ctx', 'tensor'), 'dp')
- qkv_grad: float32 [768, 3, 768], P(('dp', 'ctx'), None, 'tensor')
- proj_grad: float32 [768, 768], P(('dp', 'ctx'), 'tensor')
- up_weight_gradient: float32 [768, 3072], P(('dp', 'ctx'), 'tensor')
- down_weight_gradient: float32 [768, 3072], P(('dp', 'ctx'), 'tensor')
- gains_grad: float32 [2, 768], P(None, ('dp', 'ctx'))
- shifts_grad: float32 [4, 768], P(None, ('dp', 'ctx'))
- qv_bias_grad: float32 [2, 12, 64], P(None, 'tensor', ('dp', 'ctx'))
- up_bias_grad: float32 [24, 128], P('tensor', ('dp', 'ctx'))
- qkv_new: float32 [768, 3, 768], P(('dp', 'ctx'), None, 'tensor')
- proj_new: float32 [768, 768], P(('dp', 'ctx'), 'tensor')
- up_new: float32 [768, 3072], P(('dp', 'ctx'), 'tensor')
- down_new: float32 [768, 3072], P(('dp', 'ctx'), 'tensor')
- gains_new: float32 [2, 768], P(None, ('dp', 'ctx'))
- shifts_new: float32 [4, 768], P(None, ('dp', 'ctx'))
- qv_bias_new: float32 [2, 12, 64], P(None, 'tensor', ('dp', 'ctx'))
- up_bias_new: float32 [24, 128], P('tensor', ('dp', 'ctx'))
- qkv_first_next: float32 [768, 3, 768], P(('dp', 'ctx'), None, 'tensor')
- qkv_second_next: float32 [768, 3, 768], P(('dp', 'ctx'), None, 'tensor')
- proj_first_next: float32 [768, 768], P(('dp', 'ctx'), 'tensor')
- proj_second_next: float32 [768, 768], P(('dp', 'ctx'), 'tensor')
- up_first_next: float32 [768, 3072], P(('dp', 'ctx'), 'tensor')
- up_second_next: float32 [768, 3072], P(('dp', 'ctx'), 'tensor')
- down_first_next: float32 [768, 3072], P(('dp', 'ctx'), 'tensor')
- down_second_next: float32 [768, 3072], P(('dp', 'ctx'), 'tensor')
- gains_first_next: float32 [2, 768], P(None, ('dp', 'ctx'))
- gains_second_next: float32 [2, 768], P(None, ('dp', 'ctx'))
- shifts_first_next: float32 [4, 768], P(None, ('dp', 'ctx'))
- shifts_second_next: float32 [4, 768], P(None, ('dp', 'ctx'))
- qv_bias_first_next: float32 [2, 12, 64], P(None, 'tensor', ('dp', 'ctx'))
- qv_bias_second_next: float32 [2, 12, 64], P(None, 'tensor', ('dp', 'ctx'))
- up_bias_first_next: float32 [24, 128], P('tensor', ('dp', 'ctx'))
- up_bias_second_next: float32 [24, 128], P('tensor', ('dp', 'ctx'))
All inputs are finite; a program needn't handle non-finite values.
Results may differ from a plain program's by a relative error of at most 0.014.
Values may be sent and summed in bfloat16 or wider, within the bound.
A program may use at most 256 MiB of HBM per device.

v0:
```python
import jax
import jax.numpy as jnp
from jax import lax
from jax.sharding import PartitionSpec as P

HD = 64
STEP = 4


eps_norm = 1e-05
beta_one = 0.9
beta_two = 0.98
eps_adam = 1e-06
rate_qkv = 0.6
rate_proj = 1.2
rate_up = 0.1
rate_down = 0.15
rate_gains = 4.0
rate_shifts = 8.0
rate_query_bias = 20.0
rate_up_bias = 0.4
decay_rate = 0.01
root_half = 0.7071067811865476
density_scale = 0.3989422804014327


def normalize(values_in, gain_row, shift_row):
    center = values_in - jnp.mean(values_in, axis=-1, keepdims=True)
    inv_scale = lax.rsqrt(jnp.mean(center * center, axis=-1, keepdims=True) + eps_norm)
    normed = center * inv_scale
    return (normed, inv_scale, (normed * gain_row + shift_row).astype(jnp.bfloat16))


def normalize_back(grad_in, normed, inv_scale, gain_row):
    inner_term = grad_in * gain_row
    inner_term = (
        inner_term
        - jnp.mean(inner_term, axis=-1, keepdims=True)
        - normed * jnp.mean(inner_term * normed, axis=-1, keepdims=True)
    )
    return inv_scale * inner_term


def gelu_slope(hidden):
    return 0.5 * (
        1.0 + jax.scipy.special.erf(hidden * root_half)
    ) + hidden * density_scale * jnp.exp(-0.5 * hidden * hidden)


def adam_step(current, moment_one, moment_two, gradient, rate_value, decay_value):
    one_next = beta_one * moment_one + (1.0 - beta_one) * gradient
    two_next = beta_two * moment_two + (1.0 - beta_two) * gradient * gradient
    step_ratio = (
        one_next / (1.0 - beta_one**STEP) / (jnp.sqrt(two_next / (1.0 - beta_two**STEP)) + eps_adam)
    )
    return (current - rate_value * (step_ratio + decay_value * current), one_next, two_next)


def fetch_params(
    qkv_weight, proj_weight, up_weight, down_weight, norm_gains, shift_terms, qv_bias, up_bias
):
    return (
        lax.all_gather(qkv_weight.astype(jnp.bfloat16), ("dp", "ctx"), axis=0, tiled=True),
        lax.all_gather(proj_weight.astype(jnp.bfloat16), ("dp", "ctx"), axis=0, tiled=True),
        lax.all_gather(up_weight.astype(jnp.bfloat16), ("dp", "ctx"), axis=0, tiled=True),
        lax.all_gather(down_weight.astype(jnp.bfloat16), ("dp", "ctx"), axis=0, tiled=True),
        lax.all_gather(norm_gains.astype(jnp.bfloat16), ("dp", "ctx"), axis=1, tiled=True),
        lax.all_gather(shift_terms.astype(jnp.bfloat16), ("dp", "ctx"), axis=1, tiled=True),
        lax.all_gather(qv_bias.astype(jnp.bfloat16), ("dp", "ctx"), axis=2, tiled=True),
        lax.all_gather(up_bias.astype(jnp.bfloat16), ("dp", "ctx"), axis=1, tiled=True),
    )


def body(
    block_input,
    out_cotangent,
    qkv_weight,
    proj_weight,
    up_weight,
    down_weight,
    norm_gains,
    shift_terms,
    qv_bias,
    up_bias,
    qkv_first,
    qkv_second,
    proj_first,
    proj_second,
    up_first,
    up_second,
    down_first,
    down_second,
    gains_first,
    gains_second,
    shifts_first,
    shifts_second,
    qv_bias_first,
    qv_bias_second,
    up_bias_first,
    up_bias_second,
):
    row_count = block_input.shape[0]
    clip_count = block_input.shape[1]
    span_rows = row_count * lax.axis_size("tensor")
    frame_count = span_rows * lax.axis_size("ctx")
    score_scale = HD ** (-0.5)
    gathered = fetch_params(
        qkv_weight, proj_weight, up_weight, down_weight, norm_gains, shift_terms, qv_bias, up_bias
    )
    qkv_full = gathered[0]
    proj_full = gathered[1]
    up_weight_whole = gathered[2]
    down_weight_whole = gathered[3]
    gains_wide = gathered[4].astype(jnp.float32)
    shifts_wide = gathered[5].astype(jnp.float32)
    local_width = qkv_full.shape[2]
    head_count = local_width // HD
    hidden_local = up_weight_whole.shape[1]
    bias_query = gathered[6][0].reshape(local_width).astype(jnp.float32)
    bias_value = gathered[6][1].reshape(local_width).astype(jnp.float32)
    expand_bias = gathered[7].reshape(hidden_local).astype(jnp.float32)
    normed_one, inv_one, act_own = normalize(block_input, gains_wide[0], shifts_wide[0])
    act_one = lax.all_gather(act_own, "tensor", axis=0, tiled=True)
    projected = jnp.einsum("cbi,ito->cbto", act_one, qkv_full, preferred_element_type=jnp.float32)
    queries = (projected[:, :, 0] + bias_query).astype(jnp.bfloat16)
    keys_rows = projected[:, :, 1].astype(jnp.bfloat16)
    value_rows = (projected[:, :, 2] + bias_value).astype(jnp.bfloat16)
    query_heads = queries.reshape(span_rows, clip_count, head_count, HD)
    row_top = jnp.full((clip_count, head_count, span_rows), -jnp.inf, jnp.float32)
    row_total = jnp.zeros((clip_count, head_count, span_rows), jnp.float32)
    mix_sum = jnp.zeros((span_rows, clip_count, head_count, HD), jnp.float32)
    key_piece = lax.all_gather(keys_rows, "ctx", axis=0, tiled=True)
    value_piece = lax.all_gather(value_rows, "ctx", axis=0, tiled=True)
    local_piece_rows = key_piece.shape[0]
    for block_low in range(0, local_piece_rows, 512):
        block_high = min(local_piece_rows, block_low + 512)
        key_heads = key_piece[block_low:block_high].reshape(
            block_high - block_low, clip_count, head_count, HD
        )
        value_heads = value_piece[block_low:block_high].reshape(
            block_high - block_low, clip_count, head_count, HD
        )
        scores = (
            jnp.einsum(
                "qbhe,kbhe->bhqk", query_heads, key_heads, preferred_element_type=jnp.float32
            )
            * score_scale
        )
        new_top = jnp.maximum(row_top, jnp.max(scores, axis=-1))
        shrink = jnp.exp(row_top - new_top)
        exp_terms = jnp.exp(scores - new_top[..., None])
        row_total = row_total * shrink + jnp.sum(exp_terms, axis=-1)
        update = jnp.einsum(
            "bhqk,kbhe->qbhe",
            exp_terms,
            value_heads.astype(jnp.float32),
            preferred_element_type=jnp.float32,
        )
        mix_sum = mix_sum * jnp.transpose(shrink, (2, 0, 1))[..., None] + update
        row_top = new_top
    row_top, row_total, mix_sum = (row_top, row_total, mix_sum)
    attended = (
        (mix_sum / jnp.transpose(row_total, (2, 0, 1))[..., None])
        .reshape(span_rows, clip_count, local_width)
        .astype(jnp.bfloat16)
    )
    log_total = row_top + jnp.log(row_total)
    local_piece_rows = attended
    residual = block_input + (
        lax.psum_scatter(
            jnp.einsum(
                "cbi,oi->cbo", local_piece_rows, proj_full, preferred_element_type=jnp.float32
            ),
            "tensor",
            scatter_dimension=0,
            tiled=True,
        )
        + shifts_wide[2]
    )
    normed_two, inv_two, act_two_own = normalize(residual, gains_wide[1], shifts_wide[1])
    second_activation = lax.all_gather(act_two_own, "tensor", axis=0, tiled=True)
    hidden = (
        jnp.einsum(
            "yth,hx->ytx", second_activation, up_weight_whole, preferred_element_type=jnp.float32
        )
        + expand_bias
    )
    active_mask = (0.5 * hidden * (1.0 + jax.scipy.special.erf(hidden * root_half))).astype(
        jnp.bfloat16
    )
    local_piece_rows = active_mask
    block_output = residual + (
        lax.psum_scatter(
            jnp.einsum(
                "zud,id->zui",
                local_piece_rows,
                down_weight_whole,
                preferred_element_type=jnp.float32,
            ).astype(jnp.bfloat16),
            "tensor",
            scatter_dimension=0,
            tiled=True,
        ).astype(jnp.float32)
        + shifts_wide[3]
    )
    gathered = fetch_params(
        qkv_weight, proj_weight, up_weight, down_weight, norm_gains, shift_terms, qv_bias, up_bias
    )
    qkv_full = gathered[0]
    proj_full = gathered[1]
    up_weight_whole = gathered[2]
    down_weight_whole = gathered[3]
    gains_wide = gathered[4].astype(jnp.float32)
    gradient_row_slice = lax.all_gather(
        out_cotangent.astype(jnp.bfloat16), "tensor", axis=0, tiled=True
    )
    down_weight_gradient = jnp.einsum(
        "wzs,wzi->si", gradient_row_slice, active_mask, preferred_element_type=jnp.float32
    )
    hidden_grad = jnp.einsum(
        "hqk,ky->hqy", gradient_row_slice, down_weight_whole, preferred_element_type=jnp.float32
    ) * gelu_slope(hidden)
    hidden_local_part = hidden_grad.astype(jnp.bfloat16)
    up_weight_gradient = jnp.einsum(
        "ahg,aht->gt", second_activation, hidden_local_part, preferred_element_type=jnp.float32
    )
    local_piece_rows = hidden_local_part
    act_two_grad = lax.psum_scatter(
        jnp.einsum(
            "nok,mk->nom", local_piece_rows, up_weight_whole, preferred_element_type=jnp.float32
        ),
        "tensor",
        scatter_dimension=0,
        tiled=True,
    )
    resid_grad = out_cotangent + normalize_back(act_two_grad, normed_two, inv_two, gains_wide[1])
    resid_rows = lax.all_gather(resid_grad.astype(jnp.bfloat16), "tensor", axis=0, tiled=True)
    proj_grad = jnp.einsum("cbo,cbi->oi", resid_rows, attended, preferred_element_type=jnp.float32)
    mixed_grad = jnp.einsum(
        "cbo,oi->cbi", resid_rows, proj_full, preferred_element_type=jnp.float32
    ).astype(jnp.bfloat16)
    grad_heads = mixed_grad.reshape(span_rows, clip_count, head_count, HD)
    attended_heads = attended.reshape(span_rows, clip_count, head_count, HD)
    delta_rows = jnp.sum(
        grad_heads.astype(jnp.float32) * attended_heads.astype(jnp.float32), axis=-1
    )
    delta_sum = jnp.transpose(delta_rows, (1, 2, 0))
    query_grad = jnp.zeros((span_rows, clip_count, head_count, HD), jnp.float32)
    key_grads = jnp.zeros((frame_count, clip_count, local_width), jnp.float32)
    value_grads = jnp.zeros((frame_count, clip_count, local_width), jnp.float32)
    key_piece = lax.all_gather(keys_rows, "ctx", axis=0, tiled=True)
    value_piece = lax.all_gather(value_rows, "ctx", axis=0, tiled=True)
    local_piece_rows = key_piece.shape[0]
    for block_low in range(0, local_piece_rows, 512):
        block_high = min(local_piece_rows, block_low + 512)
        key_heads = key_piece[block_low:block_high].reshape(
            block_high - block_low, clip_count, head_count, HD
        )
        value_heads = value_piece[block_low:block_high].reshape(
            block_high - block_low, clip_count, head_count, HD
        )
        scores = (
            jnp.einsum(
                "qbhe,kbhe->bhqk", query_heads, key_heads, preferred_element_type=jnp.float32
            )
            * score_scale
        )
        prob_rows = jnp.exp(scores - log_total[..., None])
        value_part = jnp.einsum(
            "bhqk,qbhe->kbhe",
            prob_rows.astype(jnp.bfloat16),
            grad_heads,
            preferred_element_type=jnp.float32,
        )
        prob_grad = jnp.einsum(
            "qbhe,kbhe->bhqk", grad_heads, value_heads, preferred_element_type=jnp.float32
        )
        score_grad = (prob_rows * (prob_grad - delta_sum[..., None])).astype(jnp.bfloat16)
        query_grad = (
            query_grad
            + jnp.einsum(
                "bhqk,kbhe->qbhe", score_grad, key_heads, preferred_element_type=jnp.float32
            )
            * score_scale
        )
        key_part = (
            jnp.einsum(
                "bhqk,qbhe->kbhe", score_grad, query_heads, preferred_element_type=jnp.float32
            )
            * score_scale
        )
        key_grads = lax.dynamic_update_slice_in_dim(
            key_grads,
            key_part.reshape(block_high - block_low, clip_count, local_width),
            block_low,
            0,
        )
        value_grads = lax.dynamic_update_slice_in_dim(
            value_grads,
            value_part.reshape(block_high - block_low, clip_count, local_width),
            block_low,
            0,
        )
    query_grad, key_grads, value_grads = (query_grad, key_grads, value_grads)
    key_grad, value_grad = (
        lax.psum_scatter(
            key_grads.astype(jnp.bfloat16), "ctx", scatter_dimension=0, tiled=True
        ).astype(jnp.float32),
        lax.psum_scatter(
            value_grads.astype(jnp.bfloat16), "ctx", scatter_dimension=0, tiled=True
        ).astype(jnp.float32),
    )
    query_grad = query_grad.reshape(span_rows, clip_count, local_width)
    stacked = jnp.stack([query_grad, key_grad, value_grad], axis=2).astype(jnp.bfloat16)
    qkv_grad = jnp.einsum("cbi,cbto->ito", act_one, stacked, preferred_element_type=jnp.float32)
    local_piece_rows = stacked
    act_one_grad = lax.psum_scatter(
        jnp.einsum(
            "cbto,ito->cbi", local_piece_rows, qkv_full, preferred_element_type=jnp.float32
        ).astype(jnp.bfloat16),
        "tensor",
        scatter_dimension=0,
        tiled=True,
    ).astype(jnp.float32)
    input_grad = resid_grad + normalize_back(act_one_grad, normed_one, inv_one, gains_wide[0])
    gains_part = jnp.stack(
        [
            jnp.sum(act_one_grad * normed_one, axis=(0, 1)),
            jnp.sum(act_two_grad * normed_two, axis=(0, 1)),
        ]
    )
    shifts_part = jnp.stack(
        [
            jnp.sum(act_one_grad, axis=(0, 1)),
            jnp.sum(act_two_grad, axis=(0, 1)),
            jnp.sum(resid_grad, axis=(0, 1)),
            jnp.sum(out_cotangent, axis=(0, 1)),
        ]
    )
    qv_part = jnp.stack(
        [jnp.sum(query_grad, axis=(0, 1)), jnp.sum(value_grad, axis=(0, 1))]
    ).reshape(2, head_count, HD)
    up_bias_part = jnp.sum(hidden_grad, axis=(0, 1)).reshape(hidden_local // 128, 128)
    shards = (
        lax.psum_scatter(qkv_grad, ("dp", "ctx"), scatter_dimension=0, tiled=True),
        lax.psum_scatter(proj_grad, ("dp", "ctx"), scatter_dimension=0, tiled=True),
        lax.psum_scatter(up_weight_gradient, ("dp", "ctx"), scatter_dimension=0, tiled=True),
        lax.psum_scatter(down_weight_gradient, ("dp", "ctx"), scatter_dimension=0, tiled=True),
        lax.psum_scatter(gains_part, ("dp", "ctx"), scatter_dimension=1, tiled=True),
        lax.psum_scatter(shifts_part, ("dp", "ctx"), scatter_dimension=1, tiled=True),
        lax.psum_scatter(qv_part, ("dp", "ctx"), scatter_dimension=2, tiled=True),
        lax.psum_scatter(up_bias_part, ("dp", "ctx"), scatter_dimension=1, tiled=True),
    )
    gains_grad, shifts_grad = lax.psum((shards[4], shards[5]), "tensor")
    qkv_new, qkv_first_next, qkv_second_next = adam_step(
        qkv_weight, qkv_first, qkv_second, shards[0], rate_qkv, decay_rate
    )
    proj_new, proj_first_next, proj_second_next = adam_step(
        proj_weight, proj_first, proj_second, shards[1], rate_proj, decay_rate
    )
    up_new, up_first_next, up_second_next = adam_step(
        up_weight, up_first, up_second, shards[2], rate_up, decay_rate
    )
    down_new, down_first_next, down_second_next = adam_step(
        down_weight, down_first, down_second, shards[3], rate_down, decay_rate
    )
    gains_new, gains_first_next, gains_second_next = adam_step(
        norm_gains, gains_first, gains_second, gains_grad, rate_gains, 0.0
    )
    shifts_new, shifts_first_next, shifts_second_next = adam_step(
        shift_terms, shifts_first, shifts_second, shifts_grad, rate_shifts, 0.0
    )
    qv_bias_new, qv_bias_first_next, qv_bias_second_next = adam_step(
        qv_bias, qv_bias_first, qv_bias_second, shards[6], rate_query_bias, 0.0
    )
    up_bias_new, up_bias_first_next, up_bias_second_next = adam_step(
        up_bias, up_bias_first, up_bias_second, shards[7], rate_up_bias, 0.0
    )
    return (
        block_output,
        input_grad,
        shards[0],
        shards[1],
        shards[2],
        shards[3],
        gains_grad,
        shifts_grad,
        shards[6],
        shards[7],
        qkv_new,
        proj_new,
        up_new,
        down_new,
        gains_new,
        shifts_new,
        qv_bias_new,
        up_bias_new,
        qkv_first_next,
        qkv_second_next,
        proj_first_next,
        proj_second_next,
        up_first_next,
        up_second_next,
        down_first_next,
        down_second_next,
        gains_first_next,
        gains_second_next,
        shifts_first_next,
        shifts_second_next,
        qv_bias_first_next,
        qv_bias_second_next,
        up_bias_first_next,
        up_bias_second_next,
    )


def solution(mesh):
    return jax.shard_map(
        body,
        mesh=mesh,
        in_specs=(
            P(("ctx", "tensor"), "dp", None),
            P(("ctx", "tensor"), "dp", None),
            P(("dp", "ctx"), None, "tensor"),
            P(("dp", "ctx"), "tensor"),
            P(("dp", "ctx"), "tensor"),
            P(("dp", "ctx"), "tensor"),
            P(None, ("dp", "ctx")),
            P(None, ("dp", "ctx")),
            P(None, "tensor", ("dp", "ctx")),
            P("tensor", ("dp", "ctx")),
            P(("dp", "ctx"), None, "tensor"),
            P(("dp", "ctx"), None, "tensor"),
            P(("dp", "ctx"), "tensor"),
            P(("dp", "ctx"), "tensor"),
            P(("dp", "ctx"), "tensor"),
            P(("dp", "ctx"), "tensor"),
            P(("dp", "ctx"), "tensor"),
            P(("dp", "ctx"), "tensor"),
            P(None, ("dp", "ctx")),
            P(None, ("dp", "ctx")),
            P(None, ("dp", "ctx")),
            P(None, ("dp", "ctx")),
            P(None, "tensor", ("dp", "ctx")),
            P(None, "tensor", ("dp", "ctx")),
            P("tensor", ("dp", "ctx")),
            P("tensor", ("dp", "ctx")),
        ),
        out_specs=(
            P(("ctx", "tensor"), "dp", None),
            P(("ctx", "tensor"), "dp", None),
            P(("dp", "ctx"), None, "tensor"),
            P(("dp", "ctx"), "tensor"),
            P(("dp", "ctx"), "tensor"),
            P(("dp", "ctx"), "tensor"),
            P(None, ("dp", "ctx")),
            P(None, ("dp", "ctx")),
            P(None, "tensor", ("dp", "ctx")),
            P("tensor", ("dp", "ctx")),
            P(("dp", "ctx"), None, "tensor"),
            P(("dp", "ctx"), "tensor"),
            P(("dp", "ctx"), "tensor"),
            P(("dp", "ctx"), "tensor"),
            P(None, ("dp", "ctx")),
            P(None, ("dp", "ctx")),
            P(None, "tensor", ("dp", "ctx")),
            P("tensor", ("dp", "ctx")),
            P(("dp", "ctx"), None, "tensor"),
            P(("dp", "ctx"), None, "tensor"),
            P(("dp", "ctx"), "tensor"),
            P(("dp", "ctx"), "tensor"),
            P(("dp", "ctx"), "tensor"),
            P(("dp", "ctx"), "tensor"),
            P(("dp", "ctx"), "tensor"),
            P(("dp", "ctx"), "tensor"),
            P(None, ("dp", "ctx")),
            P(None, ("dp", "ctx")),
            P(None, ("dp", "ctx")),
            P(None, ("dp", "ctx")),
            P(None, "tensor", ("dp", "ctx")),
            P(None, "tensor", ("dp", "ctx")),
            P("tensor", ("dp", "ctx")),
            P("tensor", ("dp", "ctx")),
        ),
        check_vma=False,
    )
```

profile of v0, /device:TPU:0, one launch (start us, length us, event | category | flops | bytes accessed | tf_op | source)
XLA Modules:
  0.0 1328.8 jit_solution(15722973713701827479)
XLA Ops:
  10.8 33.6 %all-gather.1 = bf16[16,48,2]{1,2,0:T(2,128)(2,1)S(1)} all-gather(bf16[1,48,2]{1,2,0:T(2,128)(2,1)S(1)} %convert_bitcast_fusion.1), channel_id=1, replica_groups=mesh['dp'=4,'ctx'=4,'tensor'=2] {'dp','ctx'}, dimensions={0}, use_global_device_ids=true | all-gather | bytes 3264 | tf_op jit(solution)/shard_map/all_gather | solution.py:67
  44.6 28.5 %all-gather.2 = bf16[16,48,4]{1,2,0:T(4,128)(2,1)S(1)} all-gather(bf16[1,48,4]{1,2,0:T(4,128)(2,1)S(1)} %convert_bitcast_fusion), channel_id=1, replica_groups=mesh['dp'=4,'ctx'=4,'tensor'=2] {'dp','ctx'}, dimensions={0}, use_global_device_ids=true | all-gather | bytes 6528 | tf_op jit(solution)/shard_map/all_gather | solution.py:68
  75.9 27.7 %all-gather.13.cloned.1.call-done = bf16[384,3,768]{2,0,1:T(8,128)(2,1)} async-done(((bf16[192,3,768]{2,0,1:T(8,128)(2,1)}), bf16[384,3,768]{2,0,1:T(8,128)(2,1)}) %all-gather.13.cloned.1.call-update) | async-done | bytes 1769488 | tf_op jit(solution)/shard_map/all_gather | solution.py:123
  103.6 43.2 %all-gather.15.cloned.1.call-done = bf16[768,3,384]{2,0,1:T(8,128)(2,1)} async-done(((bf16[48,3,384]{2,0,1:T(8,128)(2,1)}), bf16[768,3,384]{2,0,1:T(8,128)(2,1)}) %all-gather.15.cloned.1.call-update) | async-done | bytes 1769488 | tf_op jit(solution)/shard_map/all_gather | solution.py:63
  154.8 32.0 %all_gather.53 = bf16[2,6,64]{1,0,2:T(2,128)(2,1)S(1)} all-gather(bf16[2,6,4]{1,0,2:T(2,128)(2,1)S(1)} %copy.186), channel_id=1, replica_groups=mesh['dp'=4,'ctx'=4,'tensor'=2] {'dp','ctx'}, dimensions={2}, use_global_device_ids=true | all-gather | bytes 1632 | tf_op jit(solution)/shard_map/all_gather | solution.py:69
  189.8 47.6 %all_gather.56 = bf16[768,384]{1,0:T(8,128)(2,1)S(1)} all-gather(bf16[48,384]{1,0:T(8,128)(2,1)S(1)} %convert_element_type.171), channel_id=1, replica_groups=mesh['dp'=4,'ctx'=4,'tensor'=2] {'dp','ctx'}, dimensions={0}, use_global_device_ids=true | all-gather | bytes 626688 | tf_op jit(solution)/shard_map/all_gather | solution.py:64
  243.2 7.1 multiply_reduce_fusion.1
  252.5 5.0 copy-done
  261.1 44.5 %all-gather.17.cloned.1.call-done = bf16[1536,3,384]{0,2,1:T(8,128)(2,1)} async-done(((bf16[384,3,384]{0,2,1:T(8,128)(2,1)}), bf16[1536,3,384]{0,2,1:T(8,128)(2,1)}) %all-gather.17.cloned.1.call-update) | async-done | bytes 3538960 | tf_op jit(solution)/shard_map/all_gather | solution.py:133
  309.0 8.3 fusion.1
  317.3 7.0 multiply_reduce_fusion
  328.5 9.8 fusion.2
  338.3 7.6 fusion.55
  351.5 44.8 %reduce-scatter.18.cloned.1.call-done = f32[192,3,768]{2,0,1:T(8,128)} async-done(((f32[384,3,768]{2,0,1:T(8,128)}), f32[192,3,768]{2,0,1:T(8,128)}) %reduce-scatter.18.cloned.1.call-update) | async-done | bytes 1769488 | tf_op jit(solution)/shard_map/reduce_scatter | solution.py:170
  404.2 34.9 %all_gather.59 = bf16[12,128]{0,1:T(8,128)(2,1)} all-gather(bf16[12,8]{0,1:T(8,128)(2,1)S(1)} %convert_element_type.174), channel_id=1, replica_groups=mesh['dp'=4,'ctx'=4,'tensor'=2] {'dp','ctx'}, dimensions={1}, use_global_device_ids=true | all-gather | bytes 3264 | tf_op jit(solution)/shard_map/all_gather | solution.py:70
  441.9 30.2 %all-gather.19.cloned.1.call-done = bf16[384,3,768]{2,0,1:T(8,128)(2,1)} async-done(((bf16[192,3,768]{2,0,1:T(8,128)(2,1)}), bf16[384,3,768]{2,0,1:T(8,128)(2,1)}) %all-gather.19.cloned.1.call-update) | async-done | bytes 1769488 | tf_op jit(solution)/shard_map/all_gather | solution.py:181
  472.1 8.1 multiply_convert_fusion.3
  480.2 23.5 %all-gather.25.cloned.1.call-done = bf16[384,3,768]{2,0,1:T(8,128)(2,1)} async-done(((bf16[192,3,768]{2,0,1:T(8,128)(2,1)}), bf16[384,3,768]{2,0,1:T(8,128)(2,1)}) %all-gather.25.cloned.1.call-update) | async-done | bytes 1769488 | tf_op jit(solution)/shard_map/all_gather | solution.py:214
  503.7 8.0 convolution_bitcast_fusion
  511.8 75.7 %reduce-scatter.36.cloned.1.call-done = f32[48,1536]{1,0:T(8,128)} async-done(((f32[768,1536]{1,0:T(8,128)}), f32[48,1536]{1,0:T(8,128)}) %reduce-scatter.36.cloned.1.call-update) | async-done | bytes 294928 | tf_op jit(solution)/shard_map/reduce_scatter | solution.py:348
  590.1 41.5 %all-gather.23.cloned.1.call-done = bf16[768,1536]{1,0:T(8,128)(2,1)} async-done(((bf16[48,1536]{1,0:T(8,128)(2,1)}), bf16[768,1536]{1,0:T(8,128)(2,1)}) %all-gather.23.cloned.1.call-update) | async-done | bytes 2359312 | tf_op jit(solution)/shard_map/all_gather | solution.py:66
  631.5 8.5 fusion.106
  646.7 6.9 fusion.62
  653.8 39.4 %reduce-scatter.22.cloned.1.call-done = f32[192,3,768]{2,0,1:T(8,128)} async-done(((f32[384,3,768]{2,0,1:T(8,128)}), f32[192,3,768]{2,0,1:T(8,128)}) %reduce-scatter.22.cloned.1.call-update) | async-done | bytes 1769488 | tf_op jit(solution)/shard_map/reduce_scatter | solution.py:228
  697.3 27.0 %reduce-scatter.20.cloned.1.call-done = bf16[192,3,768]{2,0,1:T(8,128)(2,1)} async-done(((bf16[384,3,768]{2,0,1:T(8,128)(2,1)}), bf16[192,3,768]{2,0,1:T(8,128)(2,1)}) %reduce-scatter.20.cloned.1.call-update) | async-done | bytes 884752 | tf_op jit(solution)/shard_map/reduce_scatter | solution.py:193
  732.2 28.8 %all-gather.27.cloned.1.call-done = bf16[384,3,768]{2,0,1:T(8,128)(2,1)} async-done(((bf16[192,3,768]{2,0,1:T(8,128)(2,1)}), bf16[384,3,768]{2,0,1:T(8,128)(2,1)}) %all-gather.27.cloned.1.call-update) | async-done | bytes 1769488 | tf_op jit(solution)/shard_map/all_gather | solution.py:237
  764.0 8.6 multiply_convert_fusion
  772.6 14.2 %multiply_convert_fusion.1 = bf16[3,6,384,512]{3,2,1,0:T(8,128)(2,1)} fusion(f32[3,6,384,512]{3,2,1,0:T(8,128)} %get-tuple-element.206, bf16[384,3,6,64]{0,3,2,1:T(8,128)(2,1)S(1)} %bitcast.229, bf16[512,3,6,64]{0,3,2,1:T(8,128)(2,1)S(1)} %bitcast.243, f32[3,6,384]{2,1,0:T(8,128)S(1)} %bitcast.261, f32[3,6,384]{2,1,0:T(8,128)S(1)} %copy-done.27), kind=kOutput, calls=%fused_computation.2 | convolution fusion | flops 470679552 | bytes 23353344 | tf_op jit(solution)/shard_map/qbhe,kbhe->bhqk/dot_general | solution.py:275
  786.9 6.0 multiply_convert_fusion.2
  797.7 5.4 convolution_multiply_fusion.1
  805.5 5.5 convolution_multiply_fusion.2
  820.4 8.6 fusion.16
  831.4 8.2 fusion.18
  842.0 8.3 fusion.20
  857.0 5.8 fusion.108
  862.8 5.5 fusion.107
  874.2 12.0 reduce-scatter.24.cloned.1.call-done
  886.2 68.9 %reduce-scatter.26.cloned.1.call-done = bf16[384,3,384]{2,0,1:T(8,128)(2,1)} async-done(((bf16[1536,3,384]{2,0,1:T(8,128)(2,1)}), bf16[384,3,384]{2,0,1:T(8,128)(2,1)}) %reduce-scatter.26.cloned.1.call-update) | async-done | bytes 884752 | tf_op jit(solution)/shard_map/reduce_scatter | solution.py:309
  955.1 5.8 bitcast_convert_fusion
  961.2 7.9 convolution_bitcast_fusion.1
  978.5 11.1 reduce-scatter.28.cloned.1.call-done
  998.2 6.4 convolution_bitcast_fusion.2
  1007.2 62.8 %reduce-scatter.34.cloned.1.call-done = f32[48,1536]{1,0:T(8,128)} async-done(((f32[768,1536]{1,0:T(8,128)}), f32[48,1536]{1,0:T(8,128)}) %reduce-scatter.34.cloned.1.call-update) | async-done | bytes 294928 | tf_op jit(solution)/shard_map/reduce_scatter | solution.py:347
  1074.4 56.5 %reduce-scatter.32.cloned.1.call-done = f32[48,384]{1,0:T(8,128)} async-done(((f32[768,384]{1,0:T(8,128)}), f32[48,384]{1,0:T(8,128)}) %reduce-scatter.32.cloned.1.call-update) | async-done | bytes 73744 | tf_op jit(solution)/shard_map/reduce_scatter | solution.py:346
  1138.6 61.8 %all-reduce.4 = (f32[2,6,64]{1,0,2:T(2,128)}, f32[12,128]{1,0:T(8,128)}) all-reduce(f32[2,6,64]{1,0,2:T(2,128)} %copy.159, f32[12,128]{1,0:T(8,128)} %bitcast.269), channel_id=15, replica_groups=mesh['dp'=4,'ctx'=4,'tensor'=2] {'dp','ctx'}, use_global_device_ids=true, to_apply=%region_37.0.clone | all-reduce | flops 2304 | bytes 18432
  1211.1 36.6 %reduce-scatter.40.cloned.1.call-done = f32[48,4]{1,0:T(8,128)} async-done(((f32[768,4]{1,0:T(8,128)}), f32[48,4]{1,0:T(8,128)}) %reduce-scatter.40.cloned.1.call-update) | async-done | bytes 784
  1248.5 4.9 all-reduce.5
  1256.1 63.3 %reduce-scatter.30.cloned.1.call-done = f32[48,3,384]{2,0,1:T(8,128)} async-done(((f32[768,3,384]{2,0,1:T(8,128)}), f32[48,3,384]{2,0,1:T(8,128)}) %reduce-scatter.30.cloned.1.call-update) | async-done | bytes 221200 | tf_op jit(solution)/shard_map/reduce_scatter | solution.py:345
  (291 shorter events, 158.5 us)
Async XLA Ops:
  7.2 96.4 %all-gather.13.cloned.1.call-start = ((), (), s32[]{:S(2)}) async-start(), calls=%async_computation.12 | async-start | bytes 2654208 | tf_op jit(solution)/shard_map/all_gather | solution.py:123
  10.4 64.6 %copy-start.45 = (f32[192,3]{0,1:T(4,128)}, f32[192,3]{0,1:T(4,128)S(1)}, u32[]{:S(2)}) copy-start(f32[192,3]{0,1:T(4,128)S(1)} %broadcast_multiply_fusion.5) | copy-start | bytes 6916
  10.5 64.7 %copy-start.33 = (f32[48,3,384]{2,0,1:T(8,128)S(1)}, f32[48,3,384]{2,0,1:T(8,128)}, u32[]{:S(2)}) copy-start(f32[48,3,384]{2,0,1:T(8,128)} %param.28) | copy-start | bytes 663556
  10.8 140.5 %copy-start.49 = (f32[192,3]{0,1:T(4,128)}, f32[192,3]{0,1:T(4,128)S(1)}, u32[]{:S(2)}) copy-start(f32[192,3]{0,1:T(4,128)S(1)} %add_rsqrt_fusion.1) | copy-start | bytes 6916
  44.6 106.8 %copy-start.47 = (f32[768]{0:T(1024)}, f32[768]{0:T(1024)S(1)}, u32[]{:S(2)}) copy-start(f32[768]{0:T(1024)S(1)} %get-tuple-element.149) | copy-start | bytes 9220
  75.1 71.8 %all-gather.15.cloned.1.call-start = ((), (), s32[]{:S(2)}) async-start(), calls=%async_computation.13 | async-start | bytes 1880064 | tf_op jit(solution)/shard_map/all_gather | solution.py:63
  75.8 163.6 %all-gather.29.cloned.1.call-start = ((), (), s32[]{:S(2)}) async-start(), calls=%async_computation.30 | async-start | bytes 4423680 | tf_op jit(solution)/shard_map/all_gather | solution.py:132
  154.7 35.1 %copy-start.44 = (f32[48,384]{1,0:T(8,128)S(1)}, f32[48,384]{1,0:T(8,128)}, u32[]{:S(2)}) copy-start(f32[48,384]{1,0:T(8,128)} %param.29) | copy-start | bytes 221188
  154.8 150.9 %all-gather.17.cloned.1.call-start = ((), (), s32[]{:S(2)}) async-start(), calls=%async_computation.14 | async-start | bytes 4423680 | tf_op jit(solution)/shard_map/all_gather | solution.py:133
  189.7 206.6 %reduce-scatter.18.cloned.1.call-start = ((), (), s32[]{:S(2)}) async-start(), calls=%async_computation.15 | async-start | bytes 5308416 | tf_op jit(solution)/shard_map/reduce_scatter | solution.py:170
  237.4 108.6 %copy-start.26 = (bf16[768,384]{1,0:T(8,128)(2,1)}, bf16[768,384]{1,0:T(8,128)(2,1)S(1)}, u32[]{:S(2)}) copy-start(bf16[768,384]{1,0:T(8,128)(2,1)S(1)} %all_gather.56) | copy-start | bytes 1769476
  239.4 77.8 %copy-start.3 = (bf16[384,3,6,64]{0,3,2,1:T(8,128)(2,1)}, bf16[384,3,6,64]{0,3,2,1:T(8,128)(2,1)S(1)}, u32[]{:S(2)}) copy-start(bf16[384,3,6,64]{0,3,2,1:T(8,128)(2,1)S(1)} %add_convert_fusion.1) | copy-start | bytes 2654212
  252.5 85.7 %copy-start.29 = (f32[3,6,384]{2,1,0:T(8,128)}, f32[3,6,384]{2,1,0:T(8,128)S(1)}, u32[]{:S(2)}) copy-start(f32[3,6,384]{2,1,0:T(8,128)S(1)} %get-tuple-element.203) | copy-start | bytes 82948
  261.1 77.1 %copy-start.36 = (f32[3,6,384]{2,1,0:T(8,128)}, f32[3,6,384]{2,1,0:T(8,128)S(1)}, u32[]{:S(2)}) copy-start(f32[3,6,384]{2,1,0:T(8,128)S(1)} %fusion) | copy-start | bytes 82948
  309.0 15.4 %copy-start.14 = (bf16[512,3,384]{0,2,1:T(8,128)(2,1)}, bf16[512,3,384]{0,2,1:T(8,128)(2,1)S(1)}, u32[]{:S(2)}) copy-start(bf16[512,3,384]{0,2,1:T(8,128)(2,1)S(1)} %get-tuple-element.189) | copy-start | bytes 3538948
  309.0 15.4 %slice-start.4 = ((s8[14155776]{0:T(1024)(128)(4,1)}), s8[4194304]{0:T(1024)(128)(4,1)S(1)}, s32[]{:S(2)}) async-start(s8[14155776]{0:T(1024)(128)(4,1)} %bitcast.223), calls=%async_computation.37 | async-start | bytes 8388608
  309.0 15.4 %slice-start.5 = ((s8[14155776]{0:T(1024)(128)(4,1)}), s8[4194304]{0:T(1024)(128)(4,1)S(1)}, s32[]{:S(2)}) async-start(s8[14155776]{0:T(1024)(128)(4,1)} %bitcast.223), calls=%async_computation.38 | async-start | bytes 8388608
  309.0 15.4 %slice-start.6 = ((s8[14155776]{0:T(1024)(128)(4,1)}), s8[4194304]{0:T(1024)(128)(4,1)S(1)}, s32[]{:S(2)}) async-start(s8[14155776]{0:T(1024)(128)(4,1)} %bitcast.223), calls=%async_computation.39 | async-start | bytes 8388608
  349.8 92.0 %all-gather.21.cloned.1.call-start = ((), (), s32[]{:S(2)}) async-start(), calls=%async_computation.17 | async-start | bytes 2506752 | tf_op jit(solution)/shard_map/all_gather | solution.py:65
  351.5 120.6 %all-gather.19.cloned.1.call-start = ((), (), s32[]{:S(2)}) async-start(), calls=%async_computation.16 | async-start | bytes 2654208 | tf_op jit(solution)/shard_map/all_gather | solution.py:181
  399.8 104.0 %all-gather.25.cloned.1.call-start = ((), (), s32[]{:S(2)}) async-start(), calls=%async_computation.20 | async-start | bytes 2654208 | tf_op jit(solution)/shard_map/all_gather | solution.py:214
  403.5 184.0 %reduce-scatter.36.cloned.1.call-start = ((), (), s32[]{:S(2)}) async-start(), calls=%async_computation.29 | async-start | bytes 5013504 | tf_op jit(solution)/shard_map/reduce_scatter | solution.py:348
  511.8 119.8 %all-gather.23.cloned.1.call-start = ((), (), s32[]{:S(2)}) async-start(), calls=%async_computation.18 | async-start | bytes 2506752 | tf_op jit(solution)/shard_map/all_gather | solution.py:66
  590.0 103.2 %reduce-scatter.22.cloned.1.call-start = ((), (), s32[]{:S(2)}) async-start(), calls=%async_computation.21 | async-start | bytes 5308416 | tf_op jit(solution)/shard_map/reduce_scatter | solution.py:228
  646.6 77.6 %reduce-scatter.20.cloned.1.call-start = ((), (), s32[]{:S(2)}) async-start(), calls=%async_computation.19 | async-start | bytes 2654208 | tf_op jit(solution)/shard_map/reduce_scatter | solution.py:193
  653.6 107.4 %all-gather.27.cloned.1.call-start = ((), (), s32[]{:S(2)}) async-start(), calls=%async_computation.22 | async-start | bytes 2654208 | tf_op jit(solution)/shard_map/all_gather | solution.py:237
  731.4 32.2 %copy-start.24 = (bf16[384,3,6,64]{0,3,2,1:T(8,128)(2,1)S(1)}, bf16[384,3,6,64]{0,3,2,1:T(8,128)(2,1)}, u32[]{:S(2)}) copy-start(bf16[384,3,6,64]{0,3,2,1:T(8,128)(2,1)} %copy-done.23) | copy-start | bytes 2654212
  731.4 154.8 %reduce-scatter.24.cloned.1.call-start = ((), (), s32[]{:S(2)}) async-start(), calls=%async_computation.23 | async-start | bytes 4423680 | tf_op jit(solution)/shard_map/reduce_scatter | solution.py:306
  764.0 22.9 %slice-start = ((s8[14155776]{0:T(1024)(128)(4,1)}), s8[4194304]{0:T(1024)(128)(4,1)S(1)}, s32[]{:S(2)}) async-start(s8[14155776]{0:T(1024)(128)(4,1)} %bitcast.221), calls=%async_computation.33 | async-start | bytes 8388608
  764.0 22.9 %slice-start.1 = ((s8[14155776]{0:T(1024)(128)(4,1)}), s8[4194304]{0:T(1024)(128)(4,1)S(1)}, s32[]{:S(2)}) async-start(s8[14155776]{0:T(1024)(128)(4,1)} %bitcast.221), calls=%async_computation.34 | async-start | bytes 8388608
  772.6 20.3 %copy-start.1 = (bf16[3,6,384,512]{3,2,1,0:T(8,128)(2,1)}, bf16[3,6,384,512]{3,2,1,0:T(8,128)(2,1)S(1)}, u32[]{:S(2)}) copy-start(bf16[3,6,384,512]{3,2,1,0:T(8,128)(2,1)S(1)} %multiply_convert_fusion) | copy-start | bytes 21233668
  772.6 14.2 %slice-start.2 = ((s8[14155776]{0:T(1024)(128)(4,1)}), s8[4194304]{0:T(1024)(128)(4,1)S(1)}, s32[]{:S(2)}) async-start(s8[14155776]{0:T(1024)(128)(4,1)} %bitcast.221), calls=%async_computation.35 | async-start | bytes 8388608
  772.6 14.2 %slice-start.3 = ((s8[14155776]{0:T(1024)(128)(4,1)}), s8[1572864]{0:T(1024)(128)(4,1)S(1)}, s32[]{:S(2)}) async-start(s8[14155776]{0:T(1024)(128)(4,1)} %bitcast.221), calls=%async_computation.36 | async-start | bytes 3145728
  819.7 135.4 %reduce-scatter.26.cloned.1.call-start = ((), (), s32[]{:S(2)}) async-start(), calls=%async_computation.24 | async-start | bytes 4423680 | tf_op jit(solution)/shard_map/reduce_scatter | solution.py:309
  856.9 132.7 %reduce-scatter.28.cloned.1.call-start = ((), (), s32[]{:S(2)}) async-start(), calls=%async_computation.25 | async-start | bytes 2654208 | tf_op jit(solution)/shard_map/reduce_scatter | solution.py:317
  960.9 109.0 %reduce-scatter.34.cloned.1.call-start = ((), (), s32[]{:S(2)}) async-start(), calls=%async_computation.28 | async-start | bytes 5013504 | tf_op jit(solution)/shard_map/reduce_scatter | solution.py:347
  969.2 20.4 %copy-start.46 = (f32[192,3]{0,1:T(4,128)S(1)}, f32[192,3]{0,1:T(4,128)}, u32[]{:S(2)}) copy-start(f32[192,3]{0,1:T(4,128)} %copy-done.45) | copy-start | bytes 6916
  969.2 20.4 %copy-start.48 = (f32[768]{0:T(1024)S(1)}, f32[768]{0:T(1024)}, u32[]{:S(2)}) copy-start(f32[768]{0:T(1024)} %copy-done.47) | copy-start | bytes 9220
  969.2 20.4 %copy-start.50 = (f32[192,3]{0,1:T(4,128)S(1)}, f32[192,3]{0,1:T(4,128)}, u32[]{:S(2)}) copy-start(f32[192,3]{0,1:T(4,128)} %copy-done.49) | copy-start | bytes 6916
  969.2 161.7 %reduce-scatter.32.cloned.1.call-start = ((), (), s32[]{:S(2)}) async-start(), calls=%async_computation.27 | async-start | bytes 1253376 | tf_op jit(solution)/shard_map/reduce_scatter | solution.py:346
  974.0 24.2 %copy-start.32 = (bf16[384,3,384]{2,0,1:T(8,128)(2,1)S(1)}, bf16[384,3,384]{2,0,1:T(8,128)(2,1)}, u32[]{:S(2)}) copy-start(bf16[384,3,384]{2,0,1:T(8,128)(2,1)} %reduce-scatter.26.cloned.1.call-done) | copy-start | bytes 2654212
  974.0 236.3 %reduce-scatter.38.cloned.1.call-start = ((), (), s32[]{:S(2)}) async-start(), calls=%async_computation.31 | async-start | bytes 417792
  995.1 252.6 %reduce-scatter.40.cloned.1.call-start = ((), (), s32[]{:S(2)}) async-start(), calls=%async_computation.32 | async-start | bytes 417792
  998.2 321.2 %reduce-scatter.30.cloned.1.call-start = ((), (), s32[]{:S(2)}) async-start(), calls=%async_computation.26 | async-start | bytes 3760128 | tf_op jit(solution)/shard_map/reduce_scatter | solution.py:345
  1007.1 200.2 %copy-start.6 = (f32[192,3,768]{2,0,1:T(8,128)S(1)}, f32[192,3,768]{2,0,1:T(8,128)}, u32[]{:S(2)}) copy-start(f32[192,3,768]{2,0,1:T(8,128)} %copy-done.5) | copy-start | bytes 5308420
  1207.3 47.4 %copy-start.55 = (f32[4,48]{1,0:T(4,128)S(1)}, f32[4,48]{1,0:T(4,128)}, u32[]{:S(2)}) copy-start(f32[4,48]{1,0:T(4,128)} %param.33) | copy-start | bytes 2308
  1253.4 68.1 %copy-start.56 = (f32[4,48]{1,0:T(4,128)}, f32[4,48]{1,0:T(4,128)S(1)}, u32[]{:S(2)}) copy-start(f32[4,48]{1,0:T(4,128)S(1)} %get-tuple-element.153) | copy-start | bytes 2308
  1253.4 68.1 %copy-start.57 = (f32[2,48]{1,0:T(2,128)}, f32[2,48]{1,0:T(2,128)S(1)}, u32[]{:S(2)}) copy-start(f32[2,48]{1,0:T(2,128)S(1)} %get-tuple-element.152) | copy-start | bytes 1156
  (44 other events, 211.2 us)
Sparse Core Ops, SparseCore 0:
  75.2 28.3 all-gather.12
  106.4 40.3 all-gather.14
  154.9 80.1 all-gather.28
  237.1 68.4 all-gather.16
  350.0 46.3 reduce-scatter.17
  399.3 42.2 all-gather.20
  443.8 28.1 all-gather.18
  474.3 29.4 all-gather.24
  511.9 75.5 reduce-scatter.35
  590.2 41.2 all-gather.22
  646.8 46.4 reduce-scatter.21
  696.0 28.2 reduce-scatter.19
  731.5 29.4 all-gather.26
  819.8 66.3 reduce-scatter.23
  888.4 66.6 reduce-scatter.25
  961.0 28.4 reduce-scatter.27
  994.3 75.5 reduce-scatter.33
  1074.0 56.9 reduce-scatter.31
  1134.4 54.7 reduce-scatter.37
  1193.0 54.6 reduce-scatter.39
  1252.2 67.0 reduce-scatter.29
where the time goes:
time: 1340 us; the launch traced here: 1330 us
  waiting for transfers between devices  738 us (55%)
  blocking collectives  243 us (18%)
  matrix products  188 us (14%)
  local copies, waits for them, and re-layouts  70.8 us (5%)
  other arithmetic  70 us (5%)
  between operations  17 us (1%)
    reduce_scatter x1, waiting for transfers between devices, body(): lax.psum_scatter(down_weight_gradient, ('dp', 'ctx'), scatter_dimension=0...  75.7 us
    reduce_scatter x1, waiting for transfers between devices, body(): lax.psum_scatter(value_grads.astype(jnp.bfloat16), 'ctx', scatter_dimensi...  68.9 us
    reduce_scatter x1, waiting for transfers between devices, body(): lax.psum_scatter(qkv_grad, ('dp', 'ctx'), scatter_dimension=0, tiled=True)  63.3 us
    reduce_scatter x1, waiting for transfers between devices, body(): lax.psum_scatter(up_weight_gradient, ('dp', 'ctx'), scatter_dimension=0,...  62.8 us
    unnamed x1, blocking collectives  61.8 us
    reduce_scatter x1, waiting for transfers between devices, body(): lax.psum_scatter(proj_grad, ('dp', 'ctx'), scatter_dimension=0, tiled=True)  56.5 us
    all_gather x1, blocking collectives, fetch_params(): lax.all_gather(proj_weight.astype(jnp.bfloat16), ('dp', 'ctx'), axis=0, t...  47.6 us
    reduce_scatter x1, waiting for transfers between devices, body(): lax.psum_scatter(jnp.einsum('cbi,oi->cbo', local_piece_rows, proj_full, p...  44.8 us
  transfers between devices with their start and end apart: 21, of which 18 were waited for; matrix products, arithmetic and copies ran while one was open for 12% of the time, Pallas kernels for 0%

commit v1 on v0

v1 whole, which is shorter than its diff:
```python
import functools
import math

import jax
import jax.numpy as jnp
from jax import lax
from jax.experimental import pallas as pl
from jax.experimental.pallas import tpu as pltpu
from jax.sharding import PartitionSpec as P

HD = 64
STEP = 4
F32 = jnp.float32
BF = jnp.bfloat16

eps_norm = 1e-05
beta_one = 0.9
beta_two = 0.98
eps_adam = 1e-06
rate_qkv = 0.6
rate_proj = 1.2
rate_up = 0.1
rate_down = 0.15
rate_gains = 4.0
rate_shifts = 8.0
rate_query_bias = 20.0
rate_up_bias = 0.4
decay_rate = 0.01
root_half = 0.7071067811865476
density_scale = 0.3989422804014327
score_scale = HD ** (-0.5)
MIB = 2**20


def params(limit_mib):
    return pltpu.CompilerParams(vmem_limit_bytes=limit_mib * MIB)


def mm(a, b):
    return lax.dot_general(a, b, (((1,), (0,)), ((), ())), preferred_element_type=F32)


def mm_nt(a, b):
    return lax.dot_general(a, b, (((1,), (1,)), ((), ())), preferred_element_type=F32)


def row_mean(v):
    return jnp.mean(v, axis=-1, keepdims=True)


def normed_rows(v):
    center = v - row_mean(v)
    inv = lax.rsqrt(row_mean(center * center) + eps_norm)
    return center * inv, inv


def adam_step(current, moment_one, moment_two, gradient, rate_value, decay_value):
    one_next = beta_one * moment_one + (1.0 - beta_one) * gradient
    two_next = beta_two * moment_two + (1.0 - beta_two) * gradient * gradient
    step_ratio = (
        one_next / (1.0 - beta_one**STEP) / (jnp.sqrt(two_next / (1.0 - beta_two**STEP)) + eps_adam)
    )
    return (current - rate_value * (step_ratio + decay_value * current), one_next, two_next)


def qkv_kernel(own_ref, other_ref, w_ref, rows_ref, bias_ref, q_ref, kv_ref):
    gain, shift = rows_ref[0:1, :], rows_ref[1:2, :]
    bias_q, bias_v = bias_ref[0:1, :], bias_ref[1:2, :]
    half = own_ref.shape[0]
    width = q_ref.shape[1]
    for i, ref in enumerate((own_ref, other_ref)):
        normed, _ = normed_rows(ref[...].astype(F32))
        act = (normed * gain + shift).astype(BF)
        out = mm(act, w_ref[...])
        rows = pl.ds(i * half, half)
        q = (out[:, :width] + bias_q).astype(BF)
        q_ref[rows, :] = (q.astype(F32) * score_scale).astype(BF)
        kv_ref[rows, :width] = out[:, width : 2 * width].astype(BF)
        kv_ref[rows, width:] = (out[:, 2 * width :] + bias_v).astype(BF)


def qkv_call(own, other, weight, rows, bias):
    half, _ = own.shape
    width = weight.shape[1] // 3
    return pl.pallas_call(
        qkv_kernel,
        out_shape=(
            jax.ShapeDtypeStruct((2 * half, width), BF),
            jax.ShapeDtypeStruct((2 * half, 2 * width), BF),
        ),
        compiler_params=params(32),
        cost_estimate=pl.CostEstimate(
            flops=2 * 2 * half * weight.size, bytes_accessed=4 * MIB, transcendentals=0
        ),
        name="project_qkv",
    )(own, other, weight, rows, bias)


def head_mask(shape, h):
    lane = lax.broadcasted_iota(jnp.int32, shape, 1)
    return (lane >= HD) if h else (lane < HD)


def pick(v, h):
    return jnp.where(head_mask(v.shape, h), v, jnp.zeros_like(v))


def attend_kernel(q_ref, *refs):
    k_refs, v_refs = refs[0:4], refs[4:8]
    own_ref, send_ref, lse_ref, s_scr = refs[8:]
    half = own_ref.shape[0]
    q = q_ref[...]
    n = k_refs[0].shape[0]
    v_t = [r[...].T for r in v_refs]
    parts = []
    for h in range(2):
        qh = pick(q, h)
        tops = []
        for i in range(4):
            s = mm_nt(k_refs[i][...], qh)
            s_scr[h, pl.ds(i * n, n), :] = s
            tops.append(jnp.max(s, axis=0, keepdims=True))
        top = functools.reduce(jnp.maximum, tops)
        total = jnp.zeros_like(top)
        mix = jnp.zeros((HD, q.shape[0]), F32)
        for i in range(4):
            e = jnp.exp(s_scr[h, pl.ds(i * n, n), :] - top)
            total = total + jnp.sum(e, axis=0, keepdims=True)
            mix = mix + mm(v_t[i][h * HD : (h + 1) * HD, :], e.astype(BF))
        parts.append(mix / total)
        lse_ref[0, h : h + 1, :] = top + jnp.log(total)
    o = jnp.concatenate(parts, axis=0).T.astype(BF)
    own_ref[...] = o[:half]
    send_ref[...] = o[half:]


def attend_call(q, pieces):
    rows, width = q.shape
    pairs = width // 128
    n = pieces[0].shape[0]
    half = rows // 2
    k_spec = pl.BlockSpec((n, 128), lambda p: (0, p))
    v_spec = pl.BlockSpec((n, 128), lambda p: (0, p + pairs))
    return pl.pallas_call(
        attend_kernel,
        grid=(pairs,),
        in_specs=[pl.BlockSpec((rows, 128), lambda p: (0, p))] + [k_spec] * 4 + [v_spec] * 4,
        out_specs=[
            pl.BlockSpec((half, 128), lambda p: (0, p)),
            pl.BlockSpec((half, 128), lambda p: (0, p)),
            pl.BlockSpec((1, 2, rows), lambda p: (p, 0, 0)),
        ],
        out_shape=(
            jax.ShapeDtypeStruct((half, width), BF),
            jax.ShapeDtypeStruct((half, width), BF),
            jax.ShapeDtypeStruct((pairs, 2, rows), F32),
        ),
        scratch_shapes=[pltpu.VMEM((2, 4 * n, rows), F32)],
        compiler_params=params(40),
        cost_estimate=pl.CostEstimate(
            flops=16 * rows * 4 * n * width,
            bytes_accessed=4 * MIB,
            transcendentals=pairs * 2 * rows * 4 * n,
        ),
        name="attend",
    )(q, *pieces, *pieces)


def attend_back_kernel(*refs):
    q_ref, do_own_ref, do_got_ref, o_own_ref, o_send_ref, lse_ref = refs[:6]
    k_refs, v_refs = refs[6:10], refs[10:14]
    dq_ref = refs[14]
    dk_refs, dv_refs = refs[15:19], refs[19:23]
    q = q_ref[...]
    do = jnp.concatenate([do_own_ref[...], do_got_ref[...]], axis=0)
    o = jnp.concatenate([o_own_ref[...], o_send_ref[...]], axis=0)
    prod_t = (do.astype(F32) * o.astype(F32)).T
    q_heads = [pick(q, h) for h in range(2)]
    do_heads = [pick(do, h) for h in range(2)]
    deltas = [
        jnp.sum(prod_t[h * HD : (h + 1) * HD, :], axis=0, keepdims=True) for h in range(2)
    ]
    lses = [lse_ref[0, h : h + 1, :] for h in range(2)]
    dq_t = [jnp.zeros((HD, q.shape[0]), F32) for _ in range(2)]
    for i in range(4):
        k = k_refs[i][...]
        v = v_refs[i][...]
        k_t = k.T
        dk = jnp.zeros(k.shape, F32)
        dv = jnp.zeros(k.shape, F32)
        for h in range(2):
            p = jnp.exp(mm_nt(k, q_heads[h]) - lses[h])
            dv = dv + mm(p.astype(BF), do_heads[h])
            ds = (p * (mm_nt(v, do_heads[h]) - deltas[h])).astype(BF)
            dk = dk + mm(ds, q_heads[h])
            dq_t[h] = dq_t[h] + mm(k_t[h * HD : (h + 1) * HD, :], ds)
        dk_refs[i][...] = dk.astype(BF)
        dv_refs[i][...] = dv.astype(BF)
    dq_ref[...] = (jnp.concatenate(dq_t, axis=0).T * score_scale).astype(BF)


def attend_back_call(q, do_own, do_got, o_own, o_send, lse, pieces):
    rows, width = q.shape
    pairs = width // 128
    n = pieces[0].shape[0]
    half = rows // 2
    full = pl.BlockSpec((rows, 128), lambda p: (0, p))
    part = pl.BlockSpec((half, 128), lambda p: (0, p))
    k_spec = pl.BlockSpec((n, 128), lambda p: (0, p))
    v_spec = pl.BlockSpec((n, 128), lambda p: (0, p + pairs))
    out = pl.pallas_call(
        attend_back_kernel,
        grid=(pairs,),
        in_specs=[full, part, part, part, part, pl.BlockSpec((1, 2, rows), lambda p: (p, 0, 0))]
        + [k_spec] * 4
        + [v_spec] * 4,
        out_specs=[full] + [k_spec] * 8,
        out_shape=(jax.ShapeDtypeStruct((rows, width), BF),)
        + (jax.ShapeDtypeStruct((n, width), BF),) * 8,
        compiler_params=params(40),
        cost_estimate=pl.CostEstimate(
            flops=40 * rows * 4 * n * width,
            bytes_accessed=8 * MIB,
            transcendentals=pairs * 2 * rows * 4 * n,
        ),
        name="attend_back",
    )(q, do_own, do_got, o_own, o_send, lse, *pieces, *pieces)
    return out[0], out[1:5], out[5:9]


def ffn_kernel(clips, *refs):
    o_own, o_got = refs[0:clips], refs[clips : 2 * clips]
    x_ref, gy_ref, wo_ref, up_ref, dn_ref, b1_ref, rows_ref = refs[2 * clips : 2 * clips + 7]
    outs = refs[2 * clips + 7 :]
    y_ref, d1_ref = outs[0:2]
    do_own, do_send = outs[2 : 2 + clips], outs[2 + clips : 2 + 2 * clips]
    dup_ref, ddn_ref, dwo_ref, sums_ref, db1_ref = outs[2 + 2 * clips : 7 + 2 * clips]
    proj_scr, c_scr, ct_scr, gyt_scr, y_scr, dc_scr = outs[7 + 2 * clips :]
    half = o_own[0].shape[0]
    j = pl.program_id(0)
    gain, shift = rows_ref[0:1, :], rows_ref[1:2, :]
    bias_o, bias_2 = rows_ref[2:3, :], rows_ref[3:4, :]

    @pl.when(j == 0)
    def _():
        for i in range(clips):
            rows = pl.ds(i * half, half)
            proj = mm_nt(o_own[i][...], wo_ref[0]) + mm_nt(o_got[i][...], wo_ref[1]) + bias_o
            proj_scr[rows, :] = proj
            normed, _ = normed_rows(x_ref[rows, :].astype(F32) + proj)
            c_scr[rows, :] = (normed * gain + shift).astype(BF)
        ct_scr[...] = c_scr[...].T
        gyt_scr[...] = gy_ref[...].T
        y_scr[...] = jnp.zeros_like(y_scr)
        dc_scr[...] = jnp.zeros_like(dc_scr)

    up = up_ref[0]
    dn = dn_ref[0]
    f = mm(c_scr[...], up) + b1_ref[0]
    cdf = 0.5 * (1.0 + lax.erf(f * root_half))
    u = (f * cdf).astype(BF)
    slope = cdf + f * (density_scale * jnp.exp(-0.5 * f * f))
    df = mm(gy_ref[...], dn) * slope
    dfb = df.astype(BF)
    db1_ref[0] = jnp.sum(df, axis=0, keepdims=True)
    y_scr[...] += mm_nt(u, dn)
    dc_scr[...] += mm_nt(dfb, up)
    ddn_ref[0] = mm(gyt_scr[...], u).astype(BF)
    dup_ref[0] = mm(ct_scr[...], dfb).astype(BF)

    @pl.when(j == pl.num_programs(0) - 1)
    def _():
        sum_gain = jnp.zeros_like(gain)
        sum_dc = jnp.zeros_like(gain)
        sum_dh = jnp.zeros_like(gain)
        dwo0 = jnp.zeros(wo_ref.shape[1:], F32)
        dwo1 = jnp.zeros(wo_ref.shape[1:], F32)
        for i in range(clips):
            rows = pl.ds(i * half, half)
            proj = proj_scr[rows, :]
            normed, inv = normed_rows(x_ref[rows, :].astype(F32) + proj)
            y_ref[rows, :] = (proj + y_scr[rows, :] + bias_2).astype(BF)
            dc = dc_scr[rows, :]
            t = dc * gain
            d1 = inv * (t - row_mean(t) - normed * row_mean(t * normed))
            d1_ref[rows, :] = d1
            dh = gy_ref[rows, :].astype(F32) + d1
            dy = dh.astype(BF)
            sum_gain = sum_gain + jnp.sum(dc * normed, axis=0, keepdims=True)
            sum_dc = sum_dc + jnp.sum(dc, axis=0, keepdims=True)
            sum_dh = sum_dh + jnp.sum(dh, axis=0, keepdims=True)
            do_own[i][...] = mm(dy, wo_ref[0]).astype(BF)
            do_send[i][...] = mm(dy, wo_ref[1]).astype(BF)
            dy_t = dy.T
            dwo0 = dwo0 + mm(dy_t, o_own[i][...])
            dwo1 = dwo1 + mm(dy_t, o_got[i][...])
        dwo_ref[0] = dwo0.astype(BF)
        dwo_ref[1] = dwo1.astype(BF)
        sums_ref[0:1, :] = sum_gain
        sums_ref[1:2, :] = sum_dc
        sums_ref[2:3, :] = sum_dh
        sums_ref[3:8, :] = jnp.zeros((5, sums_ref.shape[1]), F32)


def ffn_call(o_own, o_got, x, gy, wide, b1, rows):
    clips = len(o_own)
    tokens, dim = x.shape
    half, width = o_own[0].shape
    hidden = b1.shape[1]
    block = 512
    per = hidden // block
    resident = lambda shape: pl.BlockSpec(
        shape, lambda j: (0,) * len(shape), pipeline_mode=pl.Buffered(1)
    )
    up_spec = pl.BlockSpec((1, dim, block), lambda j: (j // per, 0, j % per))
    out = pl.pallas_call(
        functools.partial(ffn_kernel, clips),
        grid=(2 * per,),
        in_specs=[resident((half, width))] * (2 * clips)
        + [
            resident((tokens, dim)),
            resident((tokens, dim)),
            pl.BlockSpec(
                (2, dim, width), lambda j: (0, 0, 2 * hidden // width), pipeline_mode=pl.Buffered(1)
            ),
            up_spec,
            pl.BlockSpec((1, dim, block), lambda j: (j // per, 0, j % per + per)),
            pl.BlockSpec((1, 1, block), lambda j: (j, 0, 0)),
            resident((8, dim)),
        ],
        out_specs=[resident((tokens, dim))] * 2
        + [resident((half, width))] * (2 * clips)
        + [
            up_spec,
            up_spec,
            resident((2, dim, width)),
            resident((8, dim)),
            pl.BlockSpec((1, 1, block), lambda j: (j, 0, 0)),
        ],
        out_shape=(
            jax.ShapeDtypeStruct((tokens, dim), BF),
            jax.ShapeDtypeStruct((tokens, dim), F32),
        )
        + (jax.ShapeDtypeStruct((half, width), BF),) * (2 * clips)
        + (
            jax.ShapeDtypeStruct((2, dim, hidden), BF),
            jax.ShapeDtypeStruct((2, dim, hidden), BF),
            jax.ShapeDtypeStruct((2, dim, width), BF),
            jax.ShapeDtypeStruct((8, dim), F32),
            jax.ShapeDtypeStruct((2 * per, 1, block), F32),
        ),
        scratch_shapes=[
            pltpu.VMEM((tokens, dim), F32),
            pltpu.VMEM((tokens, dim), BF),
            pltpu.VMEM((dim, tokens), BF),
            pltpu.VMEM((dim, tokens), BF),
            pltpu.VMEM((tokens, dim), F32),
            pltpu.VMEM((tokens, dim), F32),
        ],
        compiler_params=params(56),
        cost_estimate=pl.CostEstimate(
            flops=24 * tokens * dim * hidden, bytes_accessed=30 * MIB, transcendentals=0
        ),
        name="feed_forward",
    )(*o_own, *o_got, x, gy, wide, wide, wide, b1.reshape(2 * per, 1, block), rows)
    y, d1 = out[:2]
    do_own, do_send = out[2 : 2 + clips], out[2 + clips : 2 + 2 * clips]
    dup, ddn, dwo, sums, db1 = out[2 + 2 * clips :]
    return y, d1, do_own, do_send, dup, ddn, dwo, sums, db1.reshape(2, hidden)


def back_kernel(clips, *refs):
    own_refs, got_refs = refs[0:clips], refs[clips : 2 * clips]
    dq_refs = refs[2 * clips : 3 * clips]
    dk_refs = refs[3 * clips : 4 * clips]
    dv_refs = refs[4 * clips : 5 * clips]
    w_ref, rows_ref = refs[5 * clips : 5 * clips + 2]
    outs = refs[5 * clips + 2 :]
    da_own, da_send = outs[0:clips], outs[clips : 2 * clips]
    dw_ref, sums_ref, bias_ref = outs[2 * clips : 2 * clips + 3]
    acc_scr = outs[2 * clips + 3]
    half = own_refs[0].shape[0]
    width = dq_refs[0].shape[1]
    gain, shift = rows_ref[0:1, :], rows_ref[1:2, :]
    sum_gain = jnp.zeros_like(gain)
    sum_da = jnp.zeros_like(gain)
    sum_q = jnp.zeros((1, width), F32)
    sum_v = jnp.zeros((1, width), F32)
    for i in range(clips):
        for s, (x_ref, da_ref) in enumerate(((own_refs[i], da_own[i]), (got_refs[i], da_send[i]))):
            rows = pl.ds(s * half, half)
            normed, _ = normed_rows(x_ref[...].astype(F32))
            act = normed * gain + shift
            act_t = act.astype(BF).T
            da = jnp.zeros(act.shape, F32)
            for j, ref in enumerate((dq_refs[i], dk_refs[i], dv_refs[i])):
                g = ref[rows, :]
                cols = slice(j * width, (j + 1) * width)
                da = da + mm_nt(g, w_ref[:, cols])
                part = mm(act_t, g)
                if i == 0 and s == 0:
                    acc_scr[:, cols] = part
                else:
                    acc_scr[:, cols] += part
                if j == 0:
                    sum_q = sum_q + jnp.sum(g.astype(F32), axis=0, keepdims=True)
                if j == 2:
                    sum_v = sum_v + jnp.sum(g.astype(F32), axis=0, keepdims=True)
            da_ref[...] = da.astype(BF)
            sum_gain = sum_gain + jnp.sum(da * normed, axis=0, keepdims=True)
            sum_da = sum_da + jnp.sum(da, axis=0, keepdims=True)
    dw_ref[...] = acc_scr[...].astype(BF)
    sums_ref[0:1, :] = sum_gain
    sums_ref[1:2, :] = sum_da
    sums_ref[2:8, :] = jnp.zeros((6, sums_ref.shape[1]), F32)
    bias_ref[0:1, :] = sum_q
    bias_ref[1:2, :] = sum_v
    bias_ref[2:8, :] = jnp.zeros((6, width), F32)


def back_call(x_own, x_got, dq, dk, dv, weight, rows):
    clips = len(x_own)
    half, dim = x_own[0].shape
    width = dq[0].shape[1]
    out = pl.pallas_call(
        functools.partial(back_kernel, clips),
        out_shape=(jax.ShapeDtypeStruct((half, dim), BF),) * (2 * clips)
        + (
            jax.ShapeDtypeStruct(weight.shape, BF),
            jax.ShapeDtypeStruct((8, dim), F32),
            jax.ShapeDtypeStruct((8, width), F32),
        ),
        scratch_shapes=[pltpu.VMEM(weight.shape, F32)],
        compiler_params=params(48),
        cost_estimate=pl.CostEstimate(
            flops=8 * clips * half * weight.size, bytes_accessed=16 * MIB, transcendentals=0
        ),
        name="project_back",
    )(*x_own, *x_got, *dq, *dk, *dv, weight, rows)
    return out[:clips], out[clips : 2 * clips], out[2 * clips], out[2 * clips + 1], out[2 * clips + 2]


class Links:
    def __init__(self, mesh):
        self.dp = mesh.shape["dp"]
        self.ctx = mesh.shape["ctx"]
        self.tensor = mesh.shape["tensor"]
        self.dp_bits = self.dp.bit_length() - 1
        self.ctx_bits = self.ctx.bit_length() - 1

    def flat(self, d, c, t):
        return (d * self.ctx + c) * self.tensor + t

    def move(self, value, partner):
        pairs = []
        for d in range(self.dp):
            for c in range(self.ctx):
                for t in range(self.tensor):
                    other = partner(d, c, t)
                    if other != (d, c, t):
                        pairs.append((self.flat(d, c, t), self.flat(*other)))
        return lax.ppermute(value, ("dp", "ctx", "tensor"), pairs)

    def across_x(self, value):
        return self.move(value, lambda d, c, t: (d, c, t ^ 1))

    def across_core(self, value):
        return self.move(value, lambda d, c, t: (d ^ 1, c, t))

    def across_z(self, value):
        return self.move(value, lambda d, c, t: (d, c ^ 1, t))

    def stays(self):
        d, c = lax.axis_index("dp"), lax.axis_index("ctx")
        return (d % 2) == (c // (self.ctx // 2))

    def swap(self, value):
        half = self.ctx // 2
        moved = self.move(
            value,
            lambda d, c, t: (d, c, t) if d % 2 == c // half else (d ^ 1, c ^ half, t),
        )
        return jnp.where(self.stays(), value, moved)

    def stages(self):
        out = []
        for bit in reversed(range(self.ctx_bits)):
            out.append(("ctx", bit, self.ctx_bits - 1 - bit))
        for bit in reversed(range(self.dp_bits)):
            out.append(("dp", bit, self.dp_bits - 1 - bit))
        return out

    def step(self, value, axis, bit):
        if axis == "ctx":
            return self.move(value, lambda d, c, t: (d, c ^ (1 << bit), t))
        return self.move(value, lambda d, c, t: (d ^ (1 << bit), c, t))

    def side(self, axis, bit):
        return (lax.axis_index(axis) // (1 << bit)) % 2

    def gather(self, value, both):
        shape = value.shape
        lead = 0
        for axis, bit, place in self.stages():
            if axis == "dp" and both and not lead:
                value = jnp.stack([value, self.across_x(value)])
                lead = 1
            got = self.step(value, axis, bit)
            low = self.side(axis, bit) == 0
            value = jnp.stack(
                [jnp.where(low, value, got), jnp.where(low, got, value)], axis=lead + place
            )
        shards = self.dp * self.ctx
        return value.reshape((2,) * lead + (shards * shape[0],) + shape[1:])

    def scatter(self, value, both):
        lead = 1 if both else 0
        rest = value.shape[lead + 1 :]
        value = value.reshape(
            value.shape[:lead] + (2,) * (self.dp_bits + self.ctx_bits) + rest
        )
        for axis, bit, place in reversed(self.stages()):
            if axis == "ctx" and lead:
                value = value[0] + self.across_x(value[1])
                lead = 0
            side = self.side(axis, bit)
            keep = lax.dynamic_index_in_dim(value, side, lead + place, keepdims=False)
            give = lax.dynamic_index_in_dim(value, 1 - side, lead + place, keepdims=False)
            value = keep + self.step(give, axis, bit)
        return value


def body(links, *args):
    (
        block_input,
        out_cotangent,
        qkv_weight,
        proj_weight,
        up_weight,
        down_weight,
        norm_gains,
        shift_terms,
        qv_bias,
        up_bias,
        qkv_first,
        qkv_second,
        proj_first,
        proj_second,
        up_first,
        up_second,
        down_first,
        down_second,
        gains_first,
        gains_second,
        shifts_first,
        shifts_second,
        qv_bias_first,
        qv_bias_second,
        up_bias_first,
        up_bias_second,
    ) = args
    half, clips, dim = block_input.shape
    shard = qkv_weight.shape[0]
    shards = dim // shard
    width = qkv_weight.shape[2]
    hidden = up_weight.shape[1]
    heads = width // HD

    x_home = jnp.transpose(block_input, (1, 0, 2)).astype(BF)
    gy_home = jnp.transpose(out_cotangent, (1, 0, 2)).astype(BF)
    x = links.swap(x_home)
    x_own = [x[i] for i in range(clips)]
    x_got = [links.across_x(v) for v in x_own]

    def lanes(parts):
        flat = jnp.concatenate([p.astype(BF).reshape(-1) for p in parts])
        return jnp.pad(flat, (0, shard * 128 - flat.size)).reshape(shard, 128)

    first = jnp.concatenate(
        [qkv_weight.reshape(shard, 3 * width).astype(BF), lanes([norm_gains, shift_terms, qv_bias])],
        axis=1,
    )
    second = jnp.concatenate(
        [up_weight.astype(BF), down_weight.astype(BF), proj_weight.astype(BF), lanes([up_bias])],
        axis=1,
    )
    first = links.gather(first, False)
    second = links.gather(second, True)
    w_qkv = first[:, : 3 * width]
    small = first[:, 3 * width :].reshape(shards, shard * 128)
    n_g, n_s = 2 * shard, 4 * shard
    gains = jnp.transpose(small[:, :n_g].reshape(shards, 2, shard), (1, 0, 2)).reshape(2, dim)
    shifts = jnp.transpose(
        small[:, n_g : n_g + n_s].reshape(shards, 4, shard), (1, 0, 2)
    ).reshape(4, dim)
    qv_cols = qv_bias.shape[2]
    biases = jnp.transpose(
        small[:, n_g + n_s : n_g + n_s + qv_bias.size].reshape(shards, 2, heads, qv_cols),
        (1, 2, 0, 3),
    ).reshape(2, width)
    ub_rows, ub_cols = up_bias.shape
    b1 = jnp.transpose(
        second[:, :, 2 * hidden + width :]
        .reshape(2, shards, shard * 128)[:, :, : up_bias.size]
        .reshape(2, shards, ub_rows, ub_cols),
        (0, 2, 1, 3),
    ).reshape(2, hidden)
    gains, shifts, biases, b1 = (v.astype(F32) for v in (gains, shifts, biases, b1))
    zero4 = jnp.zeros((4, dim), F32)
    rows_one = jnp.concatenate([gains[0:1], shifts[0:1], zero4, zero4[:2]])
    rows_two = jnp.concatenate([gains[1:2], shifts[1:4], zero4])
    biases = jnp.concatenate([biases, jnp.zeros((6, width), F32)])

    q, pieces, o_own, o_send, o_got, lse = [], [], [], [], [], []
    for i in range(clips):
        q_i, kv = qkv_call(x_own[i], x_got[i], w_qkv, rows_one, biases)
        kv_z = links.across_z(kv)
        kv_c = links.across_core(kv)
        kv_d = links.across_core(kv_z)
        q.append(q_i)
        pieces.append((kv, kv_c, kv_z, kv_d))
    gy = links.swap(gy_home)
    for i in range(clips):
        own, send, lse_i = attend_call(q[i], pieces[i])
        o_own.append(own)
        o_send.append(send)
        o_got.append(links.across_x(send))
        lse.append(lse_i)

    tokens = clips * half
    y, d1, do_own, do_send, d_up, d_down, d_proj, sums_two, d_b1 = ffn_call(
        o_own, o_got, x.reshape(tokens, dim), gy.reshape(tokens, dim), second, b1, rows_two
    )
    y_home = links.swap(y.reshape(clips, half, dim))
    block_output = block_input + jnp.transpose(y_home, (1, 0, 2)).astype(F32)

    grads_two = jnp.concatenate([d_up, d_down, d_proj], axis=2)
    grads_two = links.scatter(grads_two.reshape(2, shards, shard, -1), True)

    dq, dk, dv = [], [], []
    do_got = [links.across_x(v) for v in do_send]
    for i in range(clips):
        dq_i, dks, dvs = attend_back_call(
            q[i], do_own[i], do_got[i], o_own[i], o_send[i], lse[i], pieces[i]
        )
        dq.append(dq_i)
        for parts, out in ((dks, dk), (dvs, dv)):
            mine, core, z, diag = parts
            mine = mine + links.across_core(core)
            z = z + links.across_core(diag)
            out.append(mine + links.across_z(z))
    da_own, da_send, d_qkv, sums_one, sums_bias = back_call(
        x_own, x_got, dq, dk, dv, w_qkv, rows_one
    )
    grads_one = links.scatter(d_qkv.reshape(shards, shard, 3 * width), False)
    d1 = d1.reshape(clips, half, dim)
    deltas = []
    for i in range(clips):
        da = da_own[i].astype(F32) + links.across_x(da_send[i]).astype(F32)
        normed, inv = normed_rows(x_own[i].astype(F32))
        w = da * gains[0]
        deltas.append(
            (d1[i] + inv * (w - row_mean(w) - normed * row_mean(w * normed))).astype(BF)
        )
    delta_home = links.swap(jnp.stack(deltas))
    input_grad = out_cotangent + jnp.transpose(delta_home, (1, 0, 2)).astype(F32)

    cot_sum = jnp.sum(out_cotangent, axis=(0, 1))[None]
    both = jnp.concatenate(
        [sums_one[0:1], sums_two[0:1], sums_one[1:2], sums_two[1:2], sums_two[2:3], cot_sum]
    )
    both = jnp.transpose(both.reshape(6, shards, shard), (1, 0, 2)).reshape(shards, 6 * shard)
    ub = jnp.transpose(d_b1.reshape(2, ub_rows, shards, ub_cols), (0, 2, 1, 3)).reshape(
        2, shards, up_bias.size
    )
    crossed = links.across_x(jnp.concatenate([both, ub[1]], axis=1))
    qv = jnp.transpose(
        sums_bias[0:2].reshape(2, heads, shards, qv_cols), (2, 0, 1, 3)
    ).reshape(shards, qv_bias.size)
    vec = jnp.concatenate([jnp.concatenate([both, ub[0]], axis=1) + crossed, qv], axis=1)
    vec = links.scatter(vec, False)
    gains_grad = vec[:n_g].reshape(2, shard)
    shifts_grad = vec[n_g : n_g + n_s].reshape(4, shard)
    up_bias_grad = vec[6 * shard : 6 * shard + up_bias.size].reshape(up_bias.shape)
    qv_bias_grad = vec[6 * shard + up_bias.size :].reshape(qv_bias.shape)

    qkv_grad = grads_one.astype(F32).reshape(qkv_weight.shape)
    grads_two = grads_two.astype(F32)
    up_grad = grads_two[:, :hidden]
    down_grad = grads_two[:, hidden : 2 * hidden]
    proj_grad = grads_two[:, 2 * hidden :]

    qkv_next = adam_step(qkv_weight, qkv_first, qkv_second, qkv_grad, rate_qkv, decay_rate)
    proj_next = adam_step(proj_weight, proj_first, proj_second, proj_grad, rate_proj, decay_rate)
    up_next = adam_step(up_weight, up_first, up_second, up_grad, rate_up, decay_rate)
    down_next = adam_step(down_weight, down_first, down_second, down_grad, rate_down, decay_rate)
    gains_next = adam_step(norm_gains, gains_first, gains_second, gains_grad, rate_gains, 0.0)
    shifts_next = adam_step(shift_terms, shifts_first, shifts_second, shifts_grad, rate_shifts, 0.0)
    qv_next = adam_step(qv_bias, qv_bias_first, qv_bias_second, qv_bias_grad, rate_query_bias, 0.0)
    ub_next = adam_step(up_bias, up_bias_first, up_bias_second, up_bias_grad, rate_up_bias, 0.0)
    nexts = (qkv_next, proj_next, up_next, down_next, gains_next, shifts_next, qv_next, ub_next)
    return (
        block_output,
        input_grad,
        qkv_grad,
        proj_grad,
        up_grad,
        down_grad,
        gains_grad,
        shifts_grad,
        qv_bias_grad,
        up_bias_grad,
        *(n[0] for n in nexts),
        *(m for n in nexts for m in n[1:]),
    )


def solution(mesh):
    rows = P(("ctx", "tensor"), "dp", None)
    qkv = P(("dp", "ctx"), None, "tensor")
    mat = P(("dp", "ctx"), "tensor")
    norm = P(None, ("dp", "ctx"))
    qv = P(None, "tensor", ("dp", "ctx"))
    ub = P("tensor", ("dp", "ctx"))
    each = (qkv, mat, mat, mat, norm, norm, qv, ub)
    moments = tuple(s for s in each for _ in range(2))
    return jax.shard_map(
        functools.partial(body, Links(mesh)),
        mesh=mesh,
        in_specs=(rows, rows) + each + moments,
        out_specs=(rows, rows) + each + each + moments,
        check_vma=False,
    )
```

time: 1340 us -> 618 us (0.46)
  waiting for transfers between devices: 738 us -> 296 us
  blocking collectives: 243 us -> 0 us
  matrix products: 188 us -> 0 us
  Pallas kernels: 0 us -> 113 us
  starting transfers between devices: 1.51 us -> 60.8 us
  between operations: 17 us -> 3.14 us
    reduce_scatter x10 -> x0, waiting for transfers between devices: 461 us -> none  [the longest x1 75.7 us: body(): lax.psum_scatter(down_weight_gradient, ('dp', 'ctx'), scatter_dimension=0...]
    ppermute x0 -> x66, waiting for transfers between devices: none -> 296 us  [move(): return lax.ppermute(value, ('dp', 'ctx', 'tensor'), pairs)]
    all_gather x9 -> x0, waiting for transfers between devices: 239 us -> none  [the longest x1 44.5 us: body(): value_piece = lax.all_gather(value_rows, 'ctx', axis=0, tiled=True)]
    dot_general x30 -> x0, matrix products: 188 us -> none  [the longest x3 28.8 us: body(): jnp.einsum('qbhe,kbhe->bhqk', grad_heads, value_heads, preferred_element_...]
    all_gather x5 -> x0, blocking collectives: 177 us -> none  [the longest x1 47.6 us: fetch_params(): lax.all_gather(proj_weight.astype(jnp.bfloat16), ('dp', 'ctx'), axis=0, t...]
    pallas_call x0 -> x11, Pallas kernels: none -> 113 us  [the longest x3 43.4 us: attend_back_call(): pl.pallas_call(attend_back_kernel, grid=(pairs,), in_specs=[full, part, p...]
    unnamed x1 -> x0, blocking collectives: 61.8 us -> none
    ppermute x0 -> x66, starting transfers between devices: none -> 60.8 us  [move(): return lax.ppermute(value, ('dp', 'ctx', 'tensor'), pairs)]
  transfers between devices with their start and end apart: 21 -> 66, of which waited for: 18 -> 26; matrix products, arithmetic and copies ran while one was open for 12% -> 18% of each run, Pallas kernels for 0% -> 13%
where the time goes in v1:
time: 618 us; the launch traced here: 609 us
  waiting for transfers between devices  296 us (48%)
  Pallas kernels  113 us (18%)
  other arithmetic  72.9 us (12%)
  local copies, waits for them, and re-layouts  63.3 us (10%)
  starting transfers between devices  60.8 us (10%)
    ppermute x66, waiting for transfers between devices, move(): return lax.ppermute(value, ('dp', 'ctx', 'tensor'), pairs)  296 us
    ppermute x66, starting transfers between devices, move(): return lax.ppermute(value, ('dp', 'ctx', 'tensor'), pairs)  60.8 us
    pallas_call x3, Pallas kernels, attend_back_call(): pl.pallas_call(attend_back_kernel, grid=(pairs,), in_specs=[full, part, p...  43.4 us
    pallas_call x1, Pallas kernels, ffn_call(): pl.pallas_call(functools.partial(ffn_kernel, clips), grid=(2 * per,), in_...  31.7 us
    unnamed x246, local copies, waits for them, and re-layouts  23.9 us
    pallas_call x3, Pallas kernels, attend_call(): pl.pallas_call(attend_kernel, grid=(pairs,), in_specs=[pl.BlockSpec((rows...  22.7 us
    another operation x15, other arithmetic, gather(): jnp.stack([jnp.where(low, value, got), jnp.where(low, got, value)], axis=...  14.6 us
  transfers between devices with their start and end apart: 66, of which 26 were waited for; matrix products, arithmetic and copies ran while one was open for 18% of the time, Pallas kernels for 13%

profile of v1, /device:TPU:0, one launch (start us, length us, event | category | flops | bytes accessed | tf_op | source)
XLA Modules:
  0.0 609.1 jit_solution(16245322302623665500)
XLA Ops:
  4.5 4.1 collective-permute-start.21
  8.6 15.4 %collective-permute-done.21 = bf16[48,3584]{1,0:T(8,128)(2,1)S(1)} collective-permute-done((bf16[48,3584]{1,0:T(8,128)(2,1)S(1)}, bf16[48,3584]{1,0:T(8,128)(2,1)S(1)}, u32[]{:S(2)}, u32[]{:S(2)}) %collective-permute-start.21) | collective-permute-done | bytes 344096 | tf_op jit(solution)/shard_map/ppermute | solution.py:462
  25.0 15.9 %collective-permute-done.22 = bf16[2,48,3584]{2,1,0:T(8,128)(2,1)S(1)} collective-permute-done((bf16[2,48,3584]{2,1,0:T(8,128)(2,1)S(1)}, bf16[2,48,3584]{2,1,0:T(8,128)(2,1)S(1)}, u32[]{:S(2)}, u32[]{:S(2)}) %collective-permute-start.22) | collective-permute-done | bytes 688160 | tf_op jit(solution)/shard_map/ppermute | solution.py:462
  42.5 29.2 %collective-permute-done.23 = bf16[2,2,48,3584]{3,2,0,1:T(8,128)(2,1)S(1)} collective-permute-done((bf16[2,2,48,3584]{3,2,0,1:T(8,128)(2,1)S(1)}, bf16[2,2,48,3584]{3,2,0,1:T(8,128)(2,1)S(1)}, u32[]{:S(2)}, u32[]{:S(2)}) %collective-permute-start.23) | collective-permute-done | bytes 1376288 | tf_op jit(solution)/shard_map/ppermute | solution.py:462
  75.7 4.5 collective-permute-start.2
  80.2 4.4 collective-permute-done.2
  88.6 3.2 collective-permute-done.3
  93.5 43.2 %collective-permute-done.24 = bf16[2,2,2,48,3584]{4,3,1,2,0:T(8,128)(2,1)} collective-permute-done((bf16[2,2,2,48,3584]{4,3,1,2,0:T(8,128)(2,1)}, bf16[2,2,2,48,3584]{4,3,1,2,0:T(8,128)(2,1)}, u32[]{:S(2)}, u32[]{:S(2)}) %collective-permute-start.24) | collective-permute-done | bytes 2752544 | tf_op jit(solution)/shard_map/ppermute | solution.py:462
  136.7 2.0 select_bitcast_fusion.3
  138.7 3.2 pad_maximum_fusion.2
  149.8 3.6 collective-permute-done.5
  161.5 2.3 collective-permute-start.15
  168.0 2.9 collective-permute-start.14
  170.9 2.1 project_qkv.4
  174.7 2.2 broadcast_select_fusion
  179.7 6.6 %collective-permute-done.15.refs_2_.refs_6_.refs_8_.refs_12_ = bf16[384,768]{1,0:T(8,128)(2,1)} collective-permute-done((bf16[384,768]{1,0:T(8,128)(2,1)S(1)}, bf16[384,768]{1,0:T(8,128)(2,1)}, u32[]{:S(2)}, u32[]{:S(2)}) %collective-permute-start.15) | collective-permute-done | bytes 589856 | tf_op jit(solution)/shard_map/ppermute | solution.py:462
  187.0 11.9 %collective-permute-done.11.refs_2_.refs_6_.refs_8_.refs_12_ = bf16[384,768]{1,0:T(8,128)(2,1)S(1)} collective-permute-done((bf16[384,768]{1,0:T(8,128)(2,1)S(1)}, bf16[384,768]{1,0:T(8,128)(2,1)S(1)}, u32[]{:S(2)}, u32[]{:S(2)}) %collective-permute-start.11) | collective-permute-done | bytes 589856 | tf_op jit(solution)/shard_map/ppermute | solution.py:462
  200.6 10.9 %collective-permute-done.7.refs_2_.refs_6_.refs_8_.refs_12_ = bf16[384,768]{1,0:T(8,128)(2,1)S(1)} collective-permute-done((bf16[384,768]{1,0:T(8,128)(2,1)S(1)}, bf16[384,768]{1,0:T(8,128)(2,1)S(1)}, u32[]{:S(2)}, u32[]{:S(2)}) %collective-permute-start.7) | collective-permute-done | bytes 589856 | tf_op jit(solution)/shard_map/ppermute | solution.py:462
  212.1 8.2 %attend.5 = (bf16[192,384]{1,0:T(8,128)(2,1)S(1)}, bf16[192,384]{1,0:T(8,128)(2,1)S(1)}, f32[3,2,384]{2,1,0:T(2,128)S(1)}) custom-call(bf16[384,384]{1,0:T(8,128)(2,1)S(1)} %copy-done.50, bf16[384,768]{1,0:T(8,128)(2,1)S(1)} %get-tuple-element.105.refs_0_.refs_4_.refs_6_.refs_10_, ...), custom_call_target="tpu_custom_call" | custom-call | flops 3623878656 | bytes 4194304 | tf_op jit(solution)/shard_map/attend/pallas_call | solution.py:144
  221.9 7.3 %attend.4 = (bf16[192,384]{1,0:T(8,128)(2,1)S(1)}, bf16[192,384]{1,0:T(8,128)(2,1)S(1)}, f32[3,2,384]{2,1,0:T(2,128)S(1)}) custom-call(bf16[384,384]{1,0:T(8,128)(2,1)S(1)} %get-tuple-element.101.q_ref.refs_0_, bf16[384,768]{1,0:T(8,128)(2,1)S(1)} %get-tuple-element.102.refs_0_.refs_4_.refs_6_.refs_10_, ...), custom_call_target="tpu_custom_call" | custom-call | flops 3623878656 | bytes 4194304 | tf_op jit(solution)/shard_map/attend/pallas_call | solution.py:144
  230.5 7.3 %attend.3 = (bf16[192,384]{1,0:T(8,128)(2,1)S(1)}, bf16[192,384]{1,0:T(8,128)(2,1)S(1)}, f32[3,2,384]{2,1,0:T(2,128)S(1)}) custom-call(bf16[384,384]{1,0:T(8,128)(2,1)S(1)} %get-tuple-element.98.q_ref.refs_0_, bf16[384,768]{1,0:T(8,128)(2,1)S(1)} %get-tuple-element.99.refs_0_.refs_4_.refs_6_.refs_10_, ...), custom_call_target="tpu_custom_call" | custom-call | flops 3623878656 | bytes 4194304 | tf_op jit(solution)/shard_map/attend/pallas_call | solution.py:144
  239.4 3.6 select_bitcast_fusion.1
  244.2 1.8 copy.180
  246.0 4.1 copy-done.82
  251.3 31.7 %feed_forward.1 = (bf16[576,768]{1,0:T(8,128)(2,1)}, f32[576,768]{1,0:T(8,128)}, bf16[192,384]{1,0:T(8,128)(2,1)}, bf16[192,384]{1,0:T(8,128)(2,1)}, bf16[192,38...) custom-call(bf16[192,384]{1,0:T(8,128)(2,1)} %copy-done.62, ...), custom_call_target="tpu_custom_call" | custom-call | flops 16307453952 | bytes 31457280 | tf_op jit(solution)/shard_map/feed_forward/pallas_call | solution.py:316
  285.7 9.4 %pad_maximum_fusion.1 = bf16[2,768,3456]{2,1,0:T(8,128)(2,1)} fusion(bf16[2,768,384]{2,1,0:T(8,128)(2,1)} %get-tuple-element.157, bf16[2,768,1536]{2,1,0:T(8,128)(2,1)} %get-tuple-element.156, bf16[2,768,1536]{2,1,0:T(8,128)(2,1)} %get-tuple-element.155), kind=kLoop, calls=%fused_computation.1 | loop fusion | flops 31850496 | bytes 21233664 | tf_op jit(solution)/shard_map/concatenate | solution.py:637
  295.2 15.0 %attend_back.5 = (bf16[384,384]{1,0:T(8,128)(2,1)S(1)}, bf16[384,384]{1,0:T(8,128)(2,1)S(1)}, bf16[384,384]{1,0:T(8,128)(2,1)S(1)}, bf16[384,384]{1,0:T(8,128)(2...) custom-call(bf16[384,384]{1,0:T(8,128)(2,1)S(1)} %copy-done.51, ...), custom_call_target="tpu_custom_call" | custom-call | flops 9059696640 | bytes 8388608 | tf_op jit(solution)/shard_map/attend_back/pallas_call | solution.py:211
  311.8 14.1 %attend_back.4 = (bf16[384,384]{1,0:T(8,128)(2,1)S(1)}, bf16[384,384]{1,0:T(8,128)(2,1)S(1)}, bf16[384,384]{1,0:T(8,128)(2,1)S(1)}, bf16[384,384]{1,0:T(8,128)(2...) custom-call(bf16[384,384]{1,0:T(8,128)(2,1)S(1)} %copy-done.55, ...), custom_call_target="tpu_custom_call" | custom-call | flops 9059696640 | bytes 8388608 | tf_op jit(solution)/shard_map/attend_back/pallas_call | solution.py:211
  327.9 14.3 %attend_back.3 = (bf16[384,384]{1,0:T(8,128)(2,1)S(1)}, bf16[384,384]{1,0:T(8,128)(2,1)S(1)}, bf16[384,384]{1,0:T(8,128)(2,1)S(1)}, bf16[384,384]{1,0:T(8,128)(2...) custom-call(bf16[384,384]{1,0:T(8,128)(2,1)S(1)} %copy-done.53, ...), custom_call_target="tpu_custom_call" | custom-call | flops 9059696640 | bytes 8388608 | tf_op jit(solution)/shard_map/attend_back/pallas_call | solution.py:211
  346.4 8.8 %constant_dynamic-slice_fusion.5 = (bf16[2,2,1,2,2,48,3456]{6,5,4,3,2,1,0:T(8,128)(2,1)}, bf16[2,2,1,2,2,48,3456]{6,5,4,3,2,1,0:T(8,128)(2,1)}) fusion(bf16[2,2,2,2,2,48,3456]{6,5,4,3,2,1,0:T(8,128)(2,1)} %bitcast.180, s32[]{:T(128)S(6)} %select_n.291, s32[]{:T(128)S(6)} %select_n.292), kind=kLoop, calls=%fused_computation.161 | loop fusion | bytes 21233672 | tf_op jit(solution)/shard_map/jit(dynamic_index_in_dim)/dynamic_slice | solution.py:527
  368.9 5.2 copy.224
  384.2 2.4 collective-permute-done.39
  386.8 2.2 collective-permute-done.41
  389.4 5.9 collective-permute-done.38
  395.6 6.0 collective-permute-done.35
  401.7 5.4 collective-permute-done.32
  407.2 10.4 %project_back.1 = (bf16[192,768]{1,0:T(8,128)(2,1)S(1)}, bf16[192,768]{1,0:T(8,128)(2,1)S(1)}, bf16[192,768]{1,0:T(8,128)(2,1)S(1)}, bf16[192,768]{1,0:T(8,128)(...) custom-call(bf16[192,768]{1,0:T(8,128)(2,1)S(1)} %get-tuple-element., ...), custom_call_target="tpu_custom_call" | custom-call | flops 4076863488 | bytes 16777216 | tf_op jit(solution)/shard_map/project_back/pallas_call | solution.py:425
  430.1 1.9 collective-permute-start.26
  432.1 3.6 collective-permute-start.65
  435.7 2.1 dynamic-slice_bitcast_fusion.1
  439.9 16.2 %collective-permute-done.65 = f32[432]{0:T(512)S(1)} collective-permute-done((f32[432]{0:T(512)S(1)}, f32[432]{0:T(512)S(1)}, u32[]{:S(2)}, u32[]{:S(2)}) %collective-permute-start.65) | collective-permute-done | bytes 1760 | tf_op jit(solution)/shard_map/ppermute | solution.py:462
  476.7 4.6 bitcast_add_fusion
  487.5 54.5 %collective-permute-done.57 = bf16[2,2,2,48,3456]{4,3,2,1,0:T(8,128)(2,1)S(1)} collective-permute-done((bf16[2,2,2,48,3456]{4,3,2,1,0:T(8,128)(2,1)S(1)}, bf16[2,2,2,48,3456]{4,3,2,1,0:T(8,128)(2,1)S(1)}, u32[]{:S(2)}, u32[]{:S(2)}) %collective-permute-start.57) | collective-permute-done | bytes 2654240 | tf_op jit(solution)/shard_map/ppermute | solution.py:462
  547.0 4.0 collective-permute-done.53
  551.2 21.6 %collective-permute-done.58 = bf16[2,2,48,3456]{3,2,1,0:T(8,128)(2,1)S(1)} collective-permute-done((bf16[2,2,48,3456]{3,2,1,0:T(8,128)(2,1)S(1)}, bf16[2,2,48,3456]{3,2,1,0:T(8,128)(2,1)S(1)}, u32[]{:S(2)}, u32[]{:S(2)}) %collective-permute-start.58) | collective-permute-done | bytes 1327136 | tf_op jit(solution)/shard_map/ppermute | solution.py:462
  573.2 1.8 collective-permute-start.55
  575.1 15.6 %collective-permute-done.59 = bf16[2,48,3456]{2,1,0:T(8,128)(2,1)S(1)} collective-permute-done((bf16[2,48,3456]{2,1,0:T(8,128)(2,1)S(1)}, bf16[2,48,3456]{2,1,0:T(8,128)(2,1)S(1)}, u32[]{:S(2)}, u32[]{:S(2)}) %collective-permute-start.59) | collective-permute-done | bytes 663584 | tf_op jit(solution)/shard_map/ppermute | solution.py:462
  592.0 14.3 %collective-permute-done.60 = bf16[48,3456]{1,0:T(8,128)(2,1)S(1)} collective-permute-done((bf16[48,3456]{1,0:T(8,128)(2,1)S(1)}, bf16[48,3456]{1,0:T(8,128)(2,1)S(1)}, u32[]{:S(2)}, u32[]{:S(2)}) %collective-permute-start.60) | collective-permute-done | bytes 331808 | tf_op jit(solution)/shard_map/ppermute | solution.py:462
  (513 shorter events, 135.1 us)
Async XLA Ops:
  4.5 19.5 %collective-permute-start.21 = (bf16[48,3584]{1,0:T(8,128)(2,1)S(1)}, bf16[48,3584]{1,0:T(8,128)(2,1)S(1)}, u32[]{:S(2)}, u32[]{:S(2)}) collective-permute-start(bf16[48,3584]{1,0:T(8,128)(2,1)S(1)} %pad_maximum_fusion.10), channel_id=1, source_target_pairs={{0,4},{1,5},{2,6},{3,7},{4,0},{5,1},{6,2},{7,3},{8,12},{9,13},{10,... | collective-permute-start | bytes 1032200 | tf_op jit(solution)/shard_map/ppermute | solution.py:462
  24.2 16.7 %collective-permute-start.22 = (bf16[2,48,3584]{2,1,0:T(8,128)(2,1)S(1)}, bf16[2,48,3584]{2,1,0:T(8,128)(2,1)S(1)}, u32[]{:S(2)}, u32[]{:S(2)}) collective-permute-start(bf16[2,48,3584]{2,1,0:T(8,128)(2,1)S(1)} %pad_maximum_fusion.8), channel_id=1, source_target_pairs={{0,2},{1,3},{2,0},{3,1},{4,6},{5,7},{6,4},{7,5},{8,10},{9,11},{10,... | collective-permute-start | bytes 2064392 | tf_op jit(solution)/shard_map/ppermute | solution.py:462
  41.2 30.5 %collective-permute-start.23 = (bf16[2,2,48,3584]{3,2,0,1:T(8,128)(2,1)S(1)}, bf16[2,2,48,3584]{3,2,0,1:T(8,128)(2,1)S(1)}, u32[]{:S(2)}, u32[]{:S(2)}) collective-permute-start(bf16[2,2,48,3584]{3,2,0,1:T(8,128)(2,1)S(1)} %get-tuple-element.354), channel_id=1, source_target_pairs={{0,1},{1,0},{2,3},{3,2},{4,5},{5,4},{6,7},{7,6},{8,9},{9,8},{10,11... | collective-permute-start | bytes 4128776 | tf_op jit(solution)/shard_map/ppermute | solution.py:462
  73.8 62.9 %collective-permute-start.24 = (bf16[2,2,2,48,3584]{4,3,1,2,0:T(8,128)(2,1)}, bf16[2,2,2,48,3584]{4,3,1,2,0:T(8,128)(2,1)}, u32[]{:S(2)}, u32[]{:S(2)}) collective-permute-start(bf16[2,2,2,48,3584]{4,3,1,2,0:T(8,128)(2,1)} %pad_maximum_fusion.3), channel_id=1, source_target_pairs={{0,16},{1,17},{2,18},{3,19},{4,20},{5,21},{6,22},{7,23},{8,24},{9,... | collective-permute-start | bytes 8257544 | tf_op jit(solution)/shard_map/ppermute | solution.py:462
  87.1 60.4 %collective-permute-start = (bf16[3,192,768]{2,1,0:T(8,128)(2,1)}, bf16[3,192,768]{2,1,0:T(8,128)(2,1)}, u32[]{:S(2)}, u32[]{:S(2)}) collective-permute-start(bf16[3,192,768]{2,1,0:T(8,128)(2,1)} %convert_bitcast_fusion.1), channel_id=1, source_target_pairs={{4,8},{5,9},{6,10},{7,11},{8,4},{9,5},{10,6},{11,7},{20,24},{21,25... | collective-permute-start | bytes 2654216 | tf_op jit(solution)/shard_map/ppermute | solution.py:462
  92.9 50.7 %collective-permute-start.4 = (bf16[2,2,48,1280]{3,2,0,1:T(8,128)(2,1)S(1)}, bf16[2,2,48,1280]{3,2,0,1:T(8,128)(2,1)S(1)}, u32[]{:S(2)}, u32[]{:S(2)}) collective-permute-start(bf16[2,2,48,1280]{3,2,0,1:T(8,128)(2,1)S(1)} %pad_maximum_fusion.9), channel_id=1, source_target_pairs={{0,16},{1,17},{2,18},{3,19},{4,20},{5,21},{6,22},{7,23},{8,24},{9,... | collective-permute-start | bytes 1474568 | tf_op jit(solution)/shard_map/ppermute | solution.py:462
  142.7 96.7 %collective-permute-start.25 = (bf16[2,2,2,2,48,3584]{5,4,2,3,0,1:T(8,128)(2,1)}, bf16[2,2,2,2,48,3584]{5,4,2,3,0,1:T(8,128)(2,1)}, u32[]{:S(2)}, u32[]{:S(2)}) collective-permute-start(bf16[2,2,2,2,48,3584]{5,4,2,3,0,1:T(8,128)(2,1)} %pad_maximum_fusion.2), channel_id=1, source_target_pairs={{0,8},{1,9},{2,10},{3,11},{4,12},{5,13},{6,14},{7,15},{8,0},{9,1},... | collective-permute-start | bytes 16515080 | tf_op jit(solution)/shard_map/ppermute | solution.py:462
  145.8 27.3 %collective-permute-start.20 = (bf16[3,192,768]{2,1,0:T(8,128)(2,1)}, bf16[3,192,768]{2,1,0:T(8,128)(2,1)}, u32[]{:S(2)}, u32[]{:S(2)}) collective-permute-start(bf16[3,192,768]{2,1,0:T(8,128)(2,1)} %get-tuple-element.352), channel_id=1, source_target_pairs={{4,8},{5,9},{6,10},{7,11},{8,4},{9,5},{10,6},{11,7},{20,24},{21,25... | collective-permute-start | bytes 2654216 | tf_op jit(solution)/shard_map/ppermute | solution.py:462
  149.0 18.9 %collective-permute-start.9 = (bf16[192,768]{1,0:T(8,128)(2,1)S(1)}, bf16[192,768]{1,0:T(8,128)(2,1)}, u32[]{:S(2)}, u32[]{:S(2)}) collective-permute-start(bf16[192,768]{1,0:T(8,128)(2,1)S(1)} %get-tuple-element.360.own_ref.refs_1_), channel_id=1, source_target_pairs={{0,1},{1,0},{2,3},{3,2},{4,5},{5,4},{6,7},{7,6},{8,9},{9,8},{10,11... | collective-permute-start | bytes 884744 | tf_op jit(solution)/shard_map/ppermute | solution.py:462
  161.5 24.9 %collective-permute-start.15 = (bf16[384,768]{1,0:T(8,128)(2,1)S(1)}, bf16[384,768]{1,0:T(8,128)(2,1)}, u32[]{:S(2)}, u32[]{:S(2)}) collective-permute-start(bf16[384,768]{1,0:T(8,128)(2,1)S(1)} %get-tuple-element.105.refs_0_.refs_4_.refs_6_.refs_10_), channel_id=1, source_target_pairs={{0,2},{1,3},{2,0},{3,1},{4,6},{5,7},{6,4},{7,5},{8,10},{9,11},{10,... | collective-permute-start | bytes 1769480 | tf_op jit(solution)/shard_map/ppermute | solution.py:462
  168.0 18.6 %collective-permute-start.14 = (bf16[384,768]{1,0:T(8,128)(2,1)S(1)}, bf16[384,768]{1,0:T(8,128)(2,1)S(1)}, u32[]{:S(2)}, u32[]{:S(2)}) collective-permute-start(bf16[384,768]{1,0:T(8,128)(2,1)S(1)} %get-tuple-element.105.refs_0_.refs_4_.refs_6_.refs_10_), channel_id=1, source_target_pairs={{0,8},{1,9},{2,10},{3,11},{4,12},{5,13},{6,14},{7,15},{8,0},{9,1},... | collective-permute-start | bytes 1769480 | tf_op jit(solution)/shard_map/ppermute | solution.py:462
  173.0 25.9 %collective-permute-start.11 = (bf16[384,768]{1,0:T(8,128)(2,1)S(1)}, bf16[384,768]{1,0:T(8,128)(2,1)S(1)}, u32[]{:S(2)}, u32[]{:S(2)}) collective-permute-start(bf16[384,768]{1,0:T(8,128)(2,1)S(1)} %get-tuple-element.102.refs_0_.refs_4_.refs_6_.refs_10_), channel_id=1, source_target_pairs={{0,2},{1,3},{2,0},{3,1},{4,6},{5,7},{6,4},{7,5},{8,10},{9,11},{10,... | collective-permute-start | bytes 1769480 | tf_op jit(solution)/shard_map/ppermute | solution.py:462
  178.1 33.4 %collective-permute-start.7 = (bf16[384,768]{1,0:T(8,128)(2,1)S(1)}, bf16[384,768]{1,0:T(8,128)(2,1)S(1)}, u32[]{:S(2)}, u32[]{:S(2)}) collective-permute-start(bf16[384,768]{1,0:T(8,128)(2,1)S(1)} %get-tuple-element.99.refs_0_.refs_4_.refs_6_.refs_10_), channel_id=1, source_target_pairs={{0,2},{1,3},{2,0},{3,1},{4,6},{5,7},{6,4},{7,5},{8,10},{9,11},{10,... | collective-permute-start | bytes 1769480 | tf_op jit(solution)/shard_map/ppermute | solution.py:462
  186.4 25.3 %collective-permute-start.16 = (bf16[384,768]{1,0:T(8,128)(2,1)}, bf16[384,768]{1,0:T(8,128)(2,1)S(1)}, u32[]{:S(2)}, u32[]{:S(2)}) collective-permute-start(bf16[384,768]{1,0:T(8,128)(2,1)} %collective-permute-done.15.refs_2_.refs_6_.refs_8_.refs_12_), channel_id=1, source_target_pairs={{0,8},{1,9},{2,10},{3,11},{4,12},{5,13},{6,14},{7,15},{8,0},{9,1},... | collective-permute-start | bytes 1769480 | tf_op jit(solution)/shard_map/ppermute | solution.py:462
  186.6 33.7 %collective-permute-start.10 = (bf16[384,768]{1,0:T(8,128)(2,1)S(1)}, bf16[384,768]{1,0:T(8,128)(2,1)S(1)}, u32[]{:S(2)}, u32[]{:S(2)}) collective-permute-start(bf16[384,768]{1,0:T(8,128)(2,1)S(1)} %get-tuple-element.102.refs_0_.refs_4_.refs_6_.refs_10_), channel_id=1, source_target_pairs={{0,8},{1,9},{2,10},{3,11},{4,12},{5,13},{6,14},{7,15},{8,0},{9,1},... | collective-permute-start | bytes 1769480 | tf_op jit(solution)/shard_map/ppermute | solution.py:462
  198.9 22.9 %collective-permute-start.12 = (bf16[384,768]{1,0:T(8,128)(2,1)S(1)}, bf16[384,768]{1,0:T(8,128)(2,1)S(1)}, u32[]{:S(2)}, u32[]{:S(2)}) collective-permute-start(bf16[384,768]{1,0:T(8,128)(2,1)S(1)} %collective-permute-done.11.refs_2_.refs_6_.refs_8_.refs_12_), channel_id=1, source_target_pairs={{0,8},{1,9},{2,10},{3,11},{4,12},{5,13},{6,14},{7,15},{8,0},{9,1},... | collective-permute-start | bytes 1769480 | tf_op jit(solution)/shard_map/ppermute | solution.py:462
  211.5 18.9 %collective-permute-start.6 = (bf16[384,768]{1,0:T(8,128)(2,1)S(1)}, bf16[384,768]{1,0:T(8,128)(2,1)S(1)}, u32[]{:S(2)}, u32[]{:S(2)}) collective-permute-start(bf16[384,768]{1,0:T(8,128)(2,1)S(1)} %get-tuple-element.99.refs_0_.refs_4_.refs_6_.refs_10_), channel_id=1, source_target_pairs={{0,8},{1,9},{2,10},{3,11},{4,12},{5,13},{6,14},{7,15},{8,0},{9,1},... | collective-permute-start | bytes 1769480 | tf_op jit(solution)/shard_map/ppermute | solution.py:462
  211.7 18.8 %collective-permute-start.8 = (bf16[384,768]{1,0:T(8,128)(2,1)S(1)}, bf16[384,768]{1,0:T(8,128)(2,1)S(1)}, u32[]{:S(2)}, u32[]{:S(2)}) collective-permute-start(bf16[384,768]{1,0:T(8,128)(2,1)S(1)} %collective-permute-done.7.refs_2_.refs_6_.refs_8_.refs_12_), channel_id=1, source_target_pairs={{0,8},{1,9},{2,10},{3,11},{4,12},{5,13},{6,14},{7,15},{8,0},{9,1},... | collective-permute-start | bytes 1769480 | tf_op jit(solution)/shard_map/ppermute | solution.py:462
  220.3 31.0 %collective-permute-start.19 = (bf16[192,384]{1,0:T(8,128)(2,1)S(1)}, bf16[192,384]{1,0:T(8,128)(2,1)}, u32[]{:S(2)}, u32[]{:S(2)}) collective-permute-start(bf16[192,384]{1,0:T(8,128)(2,1)S(1)} %get-tuple-element.109.refs_4_), channel_id=1, source_target_pairs={{0,1},{1,0},{2,3},{3,2},{4,5},{5,4},{6,7},{7,6},{8,9},{9,8},{10,11... | collective-permute-start | bytes 442376 | tf_op jit(solution)/shard_map/ppermute | solution.py:462
  229.9 21.5 %collective-permute-start.18 = (bf16[192,384]{1,0:T(8,128)(2,1)S(1)}, bf16[192,384]{1,0:T(8,128)(2,1)}, u32[]{:S(2)}, u32[]{:S(2)}) collective-permute-start(bf16[192,384]{1,0:T(8,128)(2,1)S(1)} %get-tuple-element.108.refs_4_), channel_id=1, source_target_pairs={{0,1},{1,0},{2,3},{3,2},{4,5},{5,4},{6,7},{7,6},{8,9},{9,8},{10,11... | collective-permute-start | bytes 442376 | tf_op jit(solution)/shard_map/ppermute | solution.py:462
  237.8 13.5 %collective-permute-start.17 = (bf16[192,384]{1,0:T(8,128)(2,1)S(1)}, bf16[192,384]{1,0:T(8,128)(2,1)}, u32[]{:S(2)}, u32[]{:S(2)}) collective-permute-start(bf16[192,384]{1,0:T(8,128)(2,1)S(1)} %get-tuple-element.107.refs_4_), channel_id=1, source_target_pairs={{0,1},{1,0},{2,3},{3,2},{4,5},{5,4},{6,7},{7,6},{8,9},{9,8},{10,11... | collective-permute-start | bytes 442376 | tf_op jit(solution)/shard_map/ppermute | solution.py:462
  283.6 28.0 %collective-permute-start.28 = (bf16[192,384]{1,0:T(8,128)(2,1)}, bf16[192,384]{1,0:T(8,128)(2,1)S(1)}, u32[]{:S(2)}, u32[]{:S(2)}) collective-permute-start(bf16[192,384]{1,0:T(8,128)(2,1)} %get-tuple-element.117), channel_id=1, source_target_pairs={{0,1},{1,0},{2,3},{3,2},{4,5},{5,4},{6,7},{7,6},{8,9},{9,8},{10,11... | collective-permute-start | bytes 442376 | tf_op jit(solution)/shard_map/ppermute | solution.py:462
  285.1 42.7 %collective-permute-start.27 = (bf16[192,384]{1,0:T(8,128)(2,1)}, bf16[192,384]{1,0:T(8,128)(2,1)S(1)}, u32[]{:S(2)}, u32[]{:S(2)}) collective-permute-start(bf16[192,384]{1,0:T(8,128)(2,1)} %get-tuple-element.113), channel_id=1, source_target_pairs={{0,1},{1,0},{2,3},{3,2},{4,5},{5,4},{6,7},{7,6},{8,9},{9,8},{10,11... | collective-permute-start | bytes 442376 | tf_op jit(solution)/shard_map/ppermute | solution.py:462
  311.6 45.7 %collective-permute-start.46 = (bf16[384,384]{1,0:T(8,128)(2,1)}, bf16[384,384]{1,0:T(8,128)(2,1)}, u32[]{:S(2)}, u32[]{:S(2)}) collective-permute-start(bf16[384,384]{1,0:T(8,128)(2,1)} %get-tuple-element.147), channel_id=1, source_target_pairs={{0,8},{1,9},{2,10},{3,11},{4,12},{5,13},{6,14},{7,15},{8,0},{9,1},... | collective-permute-start | bytes 884744 | tf_op jit(solution)/shard_map/ppermute | solution.py:462
  327.4 32.3 %collective-permute-start.43 = (bf16[384,384]{1,0:T(8,128)(2,1)}, bf16[384,384]{1,0:T(8,128)(2,1)}, u32[]{:S(2)}, u32[]{:S(2)}) collective-permute-start(bf16[384,384]{1,0:T(8,128)(2,1)} %get-tuple-element.143), channel_id=1, source_target_pairs={{0,8},{1,9},{2,10},{3,11},{4,12},{5,13},{6,14},{7,15},{8,0},{9,1},... | collective-permute-start | bytes 884744 | tf_op jit(solution)/shard_map/ppermute | solution.py:462
  345.9 13.8 %collective-permute-start.40 = (bf16[384,384]{1,0:T(8,128)(2,1)}, bf16[384,384]{1,0:T(8,128)(2,1)}, u32[]{:S(2)}, u32[]{:S(2)}) collective-permute-start(bf16[384,384]{1,0:T(8,128)(2,1)} %get-tuple-element.139), channel_id=1, source_target_pairs={{0,8},{1,9},{2,10},{3,11},{4,12},{5,13},{6,14},{7,15},{8,0},{9,1},... | collective-permute-start | bytes 884744 | tf_op jit(solution)/shard_map/ppermute | solution.py:462
  345.9 17.2 %collective-permute-start.37 = (bf16[384,384]{1,0:T(8,128)(2,1)}, bf16[384,384]{1,0:T(8,128)(2,1)}, u32[]{:S(2)}, u32[]{:S(2)}) collective-permute-start(bf16[384,384]{1,0:T(8,128)(2,1)} %get-tuple-element.135), channel_id=1, source_target_pairs={{0,8},{1,9},{2,10},{3,11},{4,12},{5,13},{6,14},{7,15},{8,0},{9,1},... | collective-permute-start | bytes 884744 | tf_op jit(solution)/shard_map/ppermute | solution.py:462
  346.4 17.1 %collective-permute-start.34 = (bf16[384,384]{1,0:T(8,128)(2,1)}, bf16[384,384]{1,0:T(8,128)(2,1)}, u32[]{:S(2)}, u32[]{:S(2)}) collective-permute-start(bf16[384,384]{1,0:T(8,128)(2,1)} %get-tuple-element.131), channel_id=1, source_target_pairs={{0,8},{1,9},{2,10},{3,11},{4,12},{5,13},{6,14},{7,15},{8,0},{9,1},... | collective-permute-start | bytes 884744 | tf_op jit(solution)/shard_map/ppermute | solution.py:462
  357.3 21.2 %collective-permute-start.45 = (bf16[384,384]{1,0:T(8,128)(2,1)}, bf16[384,384]{1,0:T(8,128)(2,1)}, u32[]{:S(2)}, u32[]{:S(2)}) collective-permute-start(bf16[384,384]{1,0:T(8,128)(2,1)} %copy-done.38), channel_id=1, source_target_pairs={{0,8},{1,9},{2,10},{3,11},{4,12},{5,13},{6,14},{7,15},{8,0},{9,1},... | collective-permute-start | bytes 884744 | tf_op jit(solution)/shard_map/ppermute | solution.py:462
  359.6 17.7 %collective-permute-start.31 = (bf16[384,384]{1,0:T(8,128)(2,1)}, bf16[384,384]{1,0:T(8,128)(2,1)}, u32[]{:S(2)}, u32[]{:S(2)}) collective-permute-start(bf16[384,384]{1,0:T(8,128)(2,1)} %copy-done.42), channel_id=1, source_target_pairs={{0,8},{1,9},{2,10},{3,11},{4,12},{5,13},{6,14},{7,15},{8,0},{9,1},... | collective-permute-start | bytes 884744 | tf_op jit(solution)/shard_map/ppermute | solution.py:462
  359.6 19.4 %collective-permute-start.47 = (bf16[384,384]{1,0:T(8,128)(2,1)}, bf16[384,384]{1,0:T(8,128)(2,1)}, u32[]{:S(2)}, u32[]{:S(2)}) collective-permute-start(bf16[384,384]{1,0:T(8,128)(2,1)} %add.379), channel_id=1, source_target_pairs={{0,2},{1,3},{2,0},{3,1},{4,6},{5,7},{6,4},{7,5},{8,10},{9,11},{10,... | collective-permute-start | bytes 884744 | tf_op jit(solution)/shard_map/ppermute | solution.py:462
  363.1 18.1 %collective-permute-start.42 = (bf16[384,384]{1,0:T(8,128)(2,1)}, bf16[384,384]{1,0:T(8,128)(2,1)S(1)}, u32[]{:S(2)}, u32[]{:S(2)}) collective-permute-start(bf16[384,384]{1,0:T(8,128)(2,1)} %copy-done.39), channel_id=1, source_target_pairs={{0,8},{1,9},{2,10},{3,11},{4,12},{5,13},{6,14},{7,15},{8,0},{9,1},... | collective-permute-start | bytes 884744 | tf_op jit(solution)/shard_map/ppermute | solution.py:462
  363.5 17.7 %collective-permute-start.44 = (bf16[384,384]{1,0:T(8,128)(2,1)}, bf16[384,384]{1,0:T(8,128)(2,1)}, u32[]{:S(2)}, u32[]{:S(2)}) collective-permute-start(bf16[384,384]{1,0:T(8,128)(2,1)} %add.376), channel_id=1, source_target_pairs={{0,2},{1,3},{2,0},{3,1},{4,6},{5,7},{6,4},{7,5},{8,10},{9,11},{10,... | collective-permute-start | bytes 884744 | tf_op jit(solution)/shard_map/ppermute | solution.py:462
  377.4 99.3 %collective-permute-start.56 = (bf16[2,2,2,2,48,3456]{5,4,3,2,0,1:T(8,128)(2,1)}, bf16[2,2,2,2,48,3456]{5,4,3,2,0,1:T(8,128)(2,1)}, u32[]{:S(2)}, u32[]{:S(2)}) collective-permute-start(bf16[2,2,2,2,48,3456]{5,4,3,2,0,1:T(8,128)(2,1)} %bitcast.178), channel_id=1, source_target_pairs={{0,8},{1,9},{2,10},{3,11},{4,12},{5,13},{6,14},{7,15},{8,0},{9,1},... | collective-permute-start | bytes 15925256 | tf_op jit(solution)/shard_map/ppermute | solution.py:462
  381.2 14.0 %collective-permute-start.38 = (bf16[384,384]{1,0:T(8,128)(2,1)S(1)}, bf16[384,384]{1,0:T(8,128)(2,1)S(1)}, u32[]{:S(2)}, u32[]{:S(2)}) collective-permute-start(bf16[384,384]{1,0:T(8,128)(2,1)S(1)} %add.370), channel_id=1, source_target_pairs={{0,2},{1,3},{2,0},{3,1},{4,6},{5,7},{6,4},{7,5},{8,10},{9,11},{10,... | collective-permute-start | bytes 884744 | tf_op jit(solution)/shard_map/ppermute | solution.py:462
  430.1 112.9 %collective-permute-start.26 = (bf16[3,192,768]{2,1,0:T(8,128)(2,1)}, bf16[3,192,768]{2,1,0:T(8,128)(2,1)}, u32[]{:S(2)}, u32[]{:S(2)}) collective-permute-start(bf16[3,192,768]{2,1,0:T(8,128)(2,1)} %bitcast.196), channel_id=1, source_target_pairs={{4,8},{5,9},{6,10},{7,11},{8,4},{9,5},{10,6},{11,7},{20,24},{21,25... | collective-permute-start | bytes 2654216 | tf_op jit(solution)/shard_map/ppermute | solution.py:462
  432.1 24.0 %collective-permute-start.65 = (f32[432]{0:T(512)S(1)}, f32[432]{0:T(512)S(1)}, u32[]{:S(2)}, u32[]{:S(2)}) collective-permute-start(f32[432]{0:T(512)S(1)} %bitcast.213), channel_id=1, source_target_pairs={{0,4},{1,5},{2,6},{3,7},{4,0},{5,1},{6,2},{7,3},{8,12},{9,13},{10,... | collective-permute-start | bytes 5192 | tf_op jit(solution)/shard_map/ppermute | solution.py:462
  437.8 37.2 %collective-permute-start.48 = (bf16[192,768]{1,0:T(8,128)(2,1)S(1)}, bf16[192,768]{1,0:T(8,128)(2,1)S(1)}, u32[]{:S(2)}, u32[]{:S(2)}) collective-permute-start(bf16[192,768]{1,0:T(8,128)(2,1)S(1)} %get-tuple-element.149), channel_id=1, source_target_pairs={{0,1},{1,0},{2,3},{3,2},{4,5},{5,4},{6,7},{7,6},{8,9},{9,8},{10,11... | collective-permute-start | bytes 884744 | tf_op jit(solution)/shard_map/ppermute | solution.py:462
  439.3 35.7 %collective-permute-start.49 = (bf16[192,768]{1,0:T(8,128)(2,1)S(1)}, bf16[192,768]{1,0:T(8,128)(2,1)S(1)}, u32[]{:S(2)}, u32[]{:S(2)}) collective-permute-start(bf16[192,768]{1,0:T(8,128)(2,1)S(1)} %get-tuple-element.151), channel_id=1, source_target_pairs={{0,1},{1,0},{2,3},{3,2},{4,5},{5,4},{6,7},{7,6},{8,9},{9,8},{10,11... | collective-permute-start | bytes 884744 | tf_op jit(solution)/shard_map/ppermute | solution.py:462
  456.1 19.0 %collective-permute-start.50 = (bf16[192,768]{1,0:T(8,128)(2,1)S(1)}, bf16[192,768]{1,0:T(8,128)(2,1)S(1)}, u32[]{:S(2)}, u32[]{:S(2)}) collective-permute-start(bf16[192,768]{1,0:T(8,128)(2,1)S(1)} %get-tuple-element.153), channel_id=1, source_target_pairs={{0,1},{1,0},{2,3},{3,2},{4,5},{5,4},{6,7},{7,6},{8,9},{9,8},{10,11... | collective-permute-start | bytes 884744 | tf_op jit(solution)/shard_map/ppermute | solution.py:462
  481.6 60.4 %collective-permute-start.57 = (bf16[2,2,2,48,3456]{4,3,2,1,0:T(8,128)(2,1)S(1)}, bf16[2,2,2,48,3456]{4,3,2,1,0:T(8,128)(2,1)S(1)}, u32[]{:S(2)}, u32[]{:S(2)}) collective-permute-start(bf16[2,2,2,48,3456]{4,3,2,1,0:T(8,128)(2,1)S(1)} %dynamic-slice_bitcast_fusion), channel_id=1, source_target_pairs={{0,16},{1,17},{2,18},{3,19},{4,20},{5,21},{6,22},{7,23},{8,24},{9,... | collective-permute-start | bytes 7962632 | tf_op jit(solution)/shard_map/ppermute | solution.py:462
  484.2 61.3 %collective-permute-start.51 = (bf16[3,192,768]{2,1,0:T(8,128)(2,1)S(1)}, bf16[3,192,768]{2,1,0:T(8,128)(2,1)S(1)}, u32[]{:S(2)}, u32[]{:S(2)}) collective-permute-start(bf16[3,192,768]{2,1,0:T(8,128)(2,1)S(1)} %pad_maximum_fusion.7), channel_id=1, source_target_pairs={{4,8},{5,9},{6,10},{7,11},{8,4},{9,5},{10,6},{11,7},{20,24},{21,25... | collective-permute-start | bytes 2654216 | tf_op jit(solution)/shard_map/ppermute | solution.py:462
  486.4 64.7 %collective-permute-start.53 = (bf16[2,2,48,1152]{3,2,1,0:T(8,128)(2,1)S(1)}, bf16[2,2,48,1152]{3,2,1,0:T(8,128)(2,1)S(1)}, u32[]{:S(2)}, u32[]{:S(2)}) collective-permute-start(bf16[2,2,48,1152]{3,2,1,0:T(8,128)(2,1)S(1)} %dynamic-slice_bitcast_fusion.3), channel_id=1, source_target_pairs={{0,16},{1,17},{2,18},{3,19},{4,20},{5,21},{6,22},{7,23},{8,24},{9,... | collective-permute-start | bytes 1327112 | tf_op jit(solution)/shard_map/ppermute | solution.py:462
  542.4 30.4 %collective-permute-start.58 = (bf16[2,2,48,3456]{3,2,1,0:T(8,128)(2,1)S(1)}, bf16[2,2,48,3456]{3,2,1,0:T(8,128)(2,1)S(1)}, u32[]{:S(2)}, u32[]{:S(2)}) collective-permute-start(bf16[2,2,48,3456]{3,2,1,0:T(8,128)(2,1)S(1)} %slice_bitcast_fusion), channel_id=1, source_target_pairs={{0,1},{1,0},{2,3},{3,2},{4,5},{5,4},{6,7},{7,6},{8,9},{9,8},{10,11... | collective-permute-start | bytes 3981320 | tf_op jit(solution)/shard_map/ppermute | solution.py:462
  551.2 22.0 %collective-permute-start.54 = (bf16[2,48,1152]{2,1,0:T(8,128)(2,1)S(1)}, bf16[2,48,1152]{2,1,0:T(8,128)(2,1)S(1)}, u32[]{:S(2)}, u32[]{:S(2)}) collective-permute-start(bf16[2,48,1152]{2,1,0:T(8,128)(2,1)S(1)} %dynamic-slice_bitcast_fusion.5), channel_id=1, source_target_pairs={{0,2},{1,3},{2,0},{3,1},{4,6},{5,7},{6,4},{7,5},{8,10},{9,11},{10,... | collective-permute-start | bytes 663560 | tf_op jit(solution)/shard_map/ppermute | solution.py:462
  573.1 17.6 %collective-permute-start.59 = (bf16[2,48,3456]{2,1,0:T(8,128)(2,1)S(1)}, bf16[2,48,3456]{2,1,0:T(8,128)(2,1)S(1)}, u32[]{:S(2)}, u32[]{:S(2)}) collective-permute-start(bf16[2,48,3456]{2,1,0:T(8,128)(2,1)S(1)} %dynamic-slice_bitcast_fusion.2), channel_id=1, source_target_pairs={{0,2},{1,3},{2,0},{3,1},{4,6},{5,7},{6,4},{7,5},{8,10},{9,11},{10,... | collective-permute-start | bytes 1990664 | tf_op jit(solution)/shard_map/ppermute | solution.py:462
  573.2 17.7 %collective-permute-start.55 = (bf16[48,1152]{1,0:T(8,128)(2,1)S(1)}, bf16[48,1152]{1,0:T(8,128)(2,1)S(1)}, u32[]{:S(2)}, u32[]{:S(2)}) collective-permute-start(bf16[48,1152]{1,0:T(8,128)(2,1)S(1)} %dynamic-slice_bitcast_fusion.6), channel_id=1, source_target_pairs={{0,4},{1,5},{2,6},{3,7},{4,0},{5,1},{6,2},{7,3},{8,12},{9,13},{10,... | collective-permute-start | bytes 331784 | tf_op jit(solution)/shard_map/ppermute | solution.py:462
  590.9 15.4 %collective-permute-start.60 = (bf16[48,3456]{1,0:T(8,128)(2,1)S(1)}, bf16[48,3456]{1,0:T(8,128)(2,1)S(1)}, u32[]{:S(2)}, u32[]{:S(2)}) collective-permute-start(bf16[48,3456]{1,0:T(8,128)(2,1)S(1)} %dynamic-slice_bitcast_fusion.4), channel_id=1, source_target_pairs={{0,4},{1,5},{2,6},{3,7},{4,0},{5,1},{6,2},{7,3},{8,12},{9,13},{10,... | collective-permute-start | bytes 995336 | tf_op jit(solution)/shard_map/ppermute | solution.py:462
  (135 other events, 1718.1 us)
